TPU v7x, 128 devices: a whole 4x4x4 slice. The times are simulated.
128 devices in a mesh: seq: 16 (over z, x), tp: 8 (over y, core).
Axes of the slice: x: 4, y: 4, z: 4, core: 2. Of those that a mesh axis runs over, the one named last changes fastest.
Arguments:
- token_inputs: bfloat16 [4, 128, 5120], P(None, 'seq'), may hold values from -6 to 6
- attn_gain: float32 [5120], replicated, may hold values from 0.1 to 1.9
- w_query: bfloat16 [5120, 4096], P(None, 'tp'), may hold values from -0.078125 to 0.078125
- key_projection: bfloat16 [5120, 1024], P(None, 'tp'), may hold values from -0.078125 to 0.078125
- value_projection: bfloat16 [5120, 1024], P(None, 'tp'), may hold values from -0.078125 to 0.078125
- w_output: bfloat16 [4096, 5120], P('tp'), may hold values from -0.09375 to 0.09375
- mlp_gain: float32 [5120], replicated, may hold values from 0.1 to 1.9
- w_gate: bfloat16 [5120, 32768], P(None, ('seq', 'tp')), may hold values from -0.078125 to 0.078125
- w_up: bfloat16 [5120, 32768], P(None, ('seq', 'tp')), may hold values from -0.078125 to 0.078125
- w_down: bfloat16 [32768, 5120], P(('seq', 'tp')), may hold values from -0.03125 to 0.03125
- key_cache: bfloat16 [576, 8, 256, 128], P('seq', 'tp'), may hold values from -300 to 300
- paged_value_cache: bfloat16 [576, 8, 256, 128], P('seq', 'tp'), may hold values from -6 to 6
- cache_lengths: int32 [128], replicated, may hold values from 1 to 32768, as said below
- page_request: int32 [576], P('seq'), may hold values from -1 to 127, as said below
- page_number: int32 [576], P('seq'), may hold values from 0 to 127, as said below
- request_slot: int32 [128], replicated, may hold values from 0 to 127, each once
Outputs:
- attended: bfloat16 [4, 128, 5120], P(None, 'seq')
- layer_out: bfloat16 [4, 128, 5120], P(None, 'seq')
Inputs may be any that keep to these rules, and one draw needn't show every extreme that they name: `cache_lengths`: one request holds exactly 32768 positions. `page_request`: the pages of request r that hold its positions are numbered 0 to ceil(cache_lengths[r] / 256) - 1, and each of them is held by exactly one pool page; every other pool page is free (-1), and some page is free. `page_number`: 0 on free pages.
All inputs are finite; a program needn't handle non-finite values.
Results may differ from a plain program's by a relative error of at most 0.012.
Values may be sent and summed in bfloat16 or wider, within the bound.
A program may use at most 128 MiB of HBM per device.

v0:
```python
import math

import jax
import jax.numpy as jnp
from jax import lax
from jax.sharding import PartitionSpec as P

STEPS = 4


rope_theta = 100000000.0
norm_eps = 1e-05
masked_low = -1e30


def rms_norm(values, gain):
    floats = values.astype(jnp.float32)
    square_mean = jnp.mean(floats * floats, axis=-1, keepdims=True)
    return floats * lax.rsqrt(square_mean + norm_eps) * gain


def apply_rotary(values, token_position):
    half_dim = values.shape[-1] // 2
    exponent = jnp.arange(half_dim, dtype=jnp.float32) * (2.0 / values.shape[-1])
    inverse_freq = rope_theta ** (-exponent)
    angles = token_position.astype(jnp.float32)[:, None] * inverse_freq[None, :]
    angles = angles[:, None, :]
    cosine = jnp.cos(angles)
    sine_part = jnp.sin(angles)
    first_half = values[..., :half_dim]
    second_half = values[..., half_dim:]
    return jnp.concatenate(
        [
            first_half * cosine - second_half * sine_part,
            second_half * cosine + first_half * sine_part,
        ],
        axis=-1,
    )


def local(
    token_inputs,
    attn_gain,
    w_query,
    key_projection,
    value_projection,
    w_output,
    mlp_gain,
    w_gate,
    w_up,
    w_down,
    key_cache,
    paged_value_cache,
    cache_lengths,
    page_request,
    page_number,
    request_slot,
):
    row_count = token_inputs.shape[1]
    total_rows = row_count * lax.axis_size("seq")
    page_count = key_cache.shape[0]
    kv_local = key_cache.shape[1]
    page_size = key_cache.shape[2]
    head_dim = key_cache.shape[3]
    heads_per_group = w_query.shape[1] // (kv_local * head_dim)
    scale_factor = head_dim ** (-0.5)
    first_row = lax.axis_index("seq") * row_count
    own_rows = first_row + jnp.arange(row_count, dtype=jnp.int32)
    row_ids = jnp.arange(total_rows, dtype=jnp.int32)
    inverse_slot = jnp.zeros((total_rows,), jnp.int32).at[request_slot].set(row_ids)
    row_lengths = cache_lengths[inverse_slot[own_rows]]
    page_live = page_request >= 0
    page_req = jnp.where(page_live, page_request, 0)
    page_row = request_slot[page_req]
    token_pos = page_number[:, None] * page_size + jnp.arange(page_size, dtype=jnp.int32)[None, :]
    token_mask = page_live[:, None] & (token_pos < cache_lengths[page_req][:, None])
    block_pages = math.gcd(page_count, max(1, 1024 // page_size))
    last_live = jnp.max(jnp.where(page_live, jnp.arange(page_count, dtype=jnp.int32) + 1, 0))
    block_total = (last_live + block_pages - 1) // block_pages
    recent_keys = []
    recent_values = []
    attended_list = []
    output_list = []
    for step_index in range(STEPS):
        hidden_in = token_inputs[step_index]
        token_position = row_lengths + step_index
        normalized_input = rms_norm(hidden_in, attn_gain).astype(jnp.bfloat16)
        query_head_rows = apply_rotary(
            jnp.dot(normalized_input, w_query, preferred_element_type=jnp.float32).reshape(
                row_count, kv_local * heads_per_group, head_dim
            ),
            token_position,
        )
        query_head_rows = query_head_rows.astype(jnp.bfloat16).reshape(
            row_count, kv_local, heads_per_group, head_dim
        )
        fresh_key = apply_rotary(
            jnp.dot(normalized_input, key_projection, preferred_element_type=jnp.float32).reshape(
                row_count, kv_local, head_dim
            ),
            token_position,
        ).astype(jnp.bfloat16)
        fresh_value = (
            jnp.dot(normalized_input, value_projection, preferred_element_type=jnp.float32)
            .astype(jnp.bfloat16)
            .reshape(row_count, kv_local, head_dim)
        )
        recent_keys.append(fresh_key)
        recent_values.append(fresh_value)
        all_queries = lax.all_gather(query_head_rows, "seq", axis=0, tiled=True)

        def block_step(block_index, running):
            run_max, run_sum, run_acc = running
            block_start = block_index * block_pages
            keys_block = lax.dynamic_slice_in_dim(key_cache, block_start, block_pages, 0)
            values_block = lax.dynamic_slice_in_dim(paged_value_cache, block_start, block_pages, 0)
            rows_block = lax.dynamic_slice_in_dim(page_row, block_start, block_pages, 0)
            mask_block = lax.dynamic_slice_in_dim(token_mask, block_start, block_pages, 0)
            live_block = lax.dynamic_slice_in_dim(page_live, block_start, block_pages, 0)
            page_query = all_queries[rows_block]
            scores = (
                jnp.einsum(
                    "pkgd,pktd->pkgt", page_query, keys_block, preferred_element_type=jnp.float32
                )
                * scale_factor
            )
            token_live = mask_block[:, None, None, :]
            scores = jnp.where(token_live, scores, masked_low)
            page_max = jnp.max(scores, axis=-1)
            weights = jnp.where(token_live, jnp.exp(scores - page_max[..., None]), 0.0)
            page_sum = jnp.sum(weights, axis=-1)
            page_acc = jnp.einsum(
                "pkgt,pktd->pkgd",
                weights.astype(jnp.bfloat16),
                values_block,
                preferred_element_type=jnp.float32,
            )
            page_owner = (rows_block[None, :] == row_ids[:, None]) & live_block[None, :]
            block_max = jnp.max(
                jnp.where(page_owner[:, :, None, None], page_max[None], masked_low), axis=1
            )
            new_max = jnp.maximum(run_max, block_max)
            factor = jnp.exp(page_max - new_max[rows_block])
            old_factor = jnp.exp(run_max - new_max)
            onehot = page_owner.astype(jnp.float32)
            run_sum = run_sum * old_factor + jnp.einsum(
                "rp,pkg->rkg", onehot, page_sum * factor, precision=lax.Precision.HIGHEST
            )
            run_acc = run_acc * old_factor[..., None] + jnp.einsum(
                "rp,pkgd->rkgd",
                onehot,
                page_acc * factor[..., None],
                precision=lax.Precision.HIGHEST,
            )
            return (new_max, run_sum, run_acc)

        start_stats = (
            jnp.full((total_rows, kv_local, heads_per_group), masked_low, jnp.float32),
            jnp.zeros((total_rows, kv_local, heads_per_group), jnp.float32),
            jnp.zeros((total_rows, kv_local, heads_per_group, head_dim), jnp.float32),
        )
        local_max, local_sum, local_acc = lax.fori_loop(0, block_total, block_step, start_stats)
        global_max = lax.pmax(local_max, "seq")
        factor = jnp.exp(local_max - global_max)
        own_sum, own_acc = (
            lax.psum_scatter(local_sum * factor, "seq", scatter_dimension=0, tiled=True),
            lax.psum_scatter(local_acc * factor[..., None], "seq", scatter_dimension=0, tiled=True),
        )
        own_max = lax.dynamic_slice_in_dim(global_max, first_row, row_count, 0)
        stacked_keys = jnp.stack(recent_keys)
        stacked_values = jnp.stack(recent_values)
        recent_scores = (
            jnp.einsum(
                "rkgd,jrkd->rkgj", query_head_rows, stacked_keys, preferred_element_type=jnp.float32
            )
            * scale_factor
        )
        recent_max = jnp.max(recent_scores, axis=-1)
        recent_weights = jnp.exp(recent_scores - recent_max[..., None])
        recent_sum = jnp.sum(recent_weights, axis=-1)
        recent_acc = jnp.einsum(
            "rkgj,jrkd->rkgd",
            recent_weights.astype(jnp.bfloat16),
            stacked_values,
            preferred_element_type=jnp.float32,
        )
        total_max = jnp.maximum(own_max, recent_max)
        cache_factor = jnp.exp(own_max - total_max)
        recent_factor = jnp.exp(recent_max - total_max)
        total_sum = own_sum * cache_factor + recent_sum * recent_factor
        total_acc = own_acc * cache_factor[..., None] + recent_acc * recent_factor[..., None]
        attention = (
            (total_acc / total_sum[..., None])
            .astype(jnp.bfloat16)
            .reshape(row_count, kv_local * heads_per_group * head_dim)
        )
        head_part = jnp.dot(attention, w_output, preferred_element_type=jnp.float32)
        attended = (hidden_in.astype(jnp.float32) + lax.psum(head_part, "tp")).astype(jnp.bfloat16)
        normed_mlp = rms_norm(attended, mlp_gain).astype(jnp.bfloat16)
        row_piece = lax.all_gather(normed_mlp, "seq", axis=0, tiled=True)
        gate_proj = jnp.dot(row_piece, w_gate, preferred_element_type=jnp.float32)
        up_proj = jnp.dot(row_piece, w_up, preferred_element_type=jnp.float32)
        activation = (jax.nn.silu(gate_proj) * up_proj).astype(jnp.bfloat16)
        partial_terms = jnp.dot(activation, w_down, preferred_element_type=jnp.float32)
        summed_units = lax.psum(partial_terms, "tp")
        mlp_result = lax.psum_scatter(summed_units, "seq", scatter_dimension=0, tiled=True)
        layer_out = (attended.astype(jnp.float32) + mlp_result).astype(jnp.bfloat16)
        attended_list.append(attended)
        output_list.append(layer_out)
    return (jnp.stack(attended_list), jnp.stack(output_list))


def solution(mesh):
    in_specs = (
        P(None, "seq", None),
        P(),
        P(None, "tp"),
        P(None, "tp"),
        P(None, "tp"),
        P("tp", None),
        P(),
        P(None, ("seq", "tp")),
        P(None, ("seq", "tp")),
        P(("seq", "tp"), None),
        P("seq", "tp", None, None),
        P("seq", "tp", None, None),
        P(),
        P("seq"),
        P("seq"),
        P(),
    )
    out_specs = (P(None, "seq", None), P(None, "seq", None))
    return jax.shard_map(local, mesh=mesh, in_specs=in_specs, out_specs=out_specs, check_vma=False)
```

profile of v0, /device:TPU:1, one launch (start us, length us, event | category | flops | bytes accessed | tf_op | source)
XLA Modules:
  0.0 1077.0 jit_solution(16876688499901593461)
XLA Ops:
  18.9 7.9 copy.259
  31.7 20.6 %all_gather.24 = bf16[128,1,4,128]{3,0,2,1:T(8,128)(2,1)S(1)} all-gather(bf16[8,1,4,128]{3,0,2,1:T(8,128)(2,1)S(1)} %pad_maximum_fusion.2), channel_id=1, replica_groups=mesh['seq'=16,'tp'=8] {'seq'}, dimensions={0}, use_global_device_ids=true | all-gather | bytes 139264 | tf_op jit(solution)/shard_map/all_gather | solution.py:110
  53.2 48.7 %while.60 = (s32[]{:T(128)}, f32[128,1,4]{0,2,1:T(4,128)S(1)}, f32[128,1,4]{0,2,1:T(4,128)S(1)}, f32[128,1,4,128]{3,0,2,1:T(8,128)S(1)}, s32[]{:T(128)}, /*index...) while((s32[]{:T(128)}, f32[128,1,4]{0,2,1:T(4,128)S(1)}, ...), condition=%wide.region_7.8_spmd.clone, body=%wide.region_3.7_spmd.clone.sunk | while | flops 5445650 | bytes 1167499 | solution.py:162
  106.0 17.2 %all_gather.25 = bf16[128,1,4,128]{3,0,2,1:T(8,128)(2,1)S(1)} all-gather(bf16[8,1,4,128]{3,0,2,1:T(8,128)(2,1)S(1)} %pad_maximum_fusion.4), channel_id=1, replica_groups=mesh['seq'=16,'tp'=8] {'seq'}, dimensions={0}, use_global_device_ids=true | all-gather | bytes 139264 | tf_op jit(solution)/shard_map/all_gather | solution.py:110
  123.4 48.7 %while.61 = (s32[]{:T(128)}, f32[128,1,4]{0,2,1:T(4,128)S(1)}, f32[128,1,4]{0,2,1:T(4,128)S(1)}, f32[128,1,4,128]{3,0,2,1:T(8,128)S(1)}, s32[]{:T(128)}, /*index...) while((s32[]{:T(128)}, f32[128,1,4]{0,2,1:T(4,128)S(1)}, ...), condition=%wide.region_17.18_spmd.clone, body=%wide.region_13.17_spmd.clone.sunk | while | flops 5445650 | bytes 1167499 | solution.py:162
  176.4 16.2 %all_gather.26 = bf16[128,1,4,128]{3,0,2,1:T(8,128)(2,1)S(1)} all-gather(bf16[8,1,4,128]{3,0,2,1:T(8,128)(2,1)S(1)} %pad_maximum_fusion.6), channel_id=1, replica_groups=mesh['seq'=16,'tp'=8] {'seq'}, dimensions={0}, use_global_device_ids=true | all-gather | bytes 139264 | tf_op jit(solution)/shard_map/all_gather | solution.py:110
  193.4 70.1 %while.62 = (s32[]{:T(128)}, f32[128,1,4]{0,2,1:T(4,128)S(1)}, f32[128,1,4]{0,2,1:T(4,128)S(1)}, f32[128,1,4,128]{3,0,2,1:T(8,128)S(1)}, s32[]{:T(128)}, /*index...) while((s32[]{:T(128)}, f32[128,1,4]{0,2,1:T(4,128)S(1)}, ...), condition=%wide.region_29.30_spmd.clone, body=%wide.region_25.29_spmd.clone.sunk | while | flops 5445650 | bytes 1167499 | solution.py:162
  267.7 17.2 %all_gather.27 = bf16[128,1,4,128]{3,0,2,1:T(8,128)(2,1)S(1)} all-gather(bf16[8,1,4,128]{3,0,2,1:T(8,128)(2,1)S(1)} %pad_maximum_fusion.8), channel_id=1, replica_groups=mesh['seq'=16,'tp'=8] {'seq'}, dimensions={0}, use_global_device_ids=true | all-gather | bytes 139264 | tf_op jit(solution)/shard_map/all_gather | solution.py:110
  285.7 70.0 %while.63 = (s32[]{:T(128)}, f32[128,1,4]{0,2,1:T(4,128)S(1)}, f32[128,1,4]{0,2,1:T(4,128)S(1)}, f32[128,1,4,128]{3,0,2,1:T(8,128)S(1)}, s32[]{:T(128)}, /*index...) while((s32[]{:T(128)}, f32[128,1,4]{0,2,1:T(4,128)S(1)}, ...), condition=%wide.region_41.42_spmd.clone, body=%wide.region_37.41_spmd.clone.sunk | while | flops 5445650 | bytes 1167499 | solution.py:162
  355.8 29.0 %all-reduce.14 = (f32[128,1,4]{0,2,1:T(4,128)S(1)}, f32[128,1,4]{0,2,1:T(4,128)S(1)}, f32[128,1,4]{0,2,1:T(4,128)S(1)}, f32[128,1,4]{0,2,1:T(4,128)S(1)}) all-reduce(f32[128,1,4]{0,2,1:T(4,128)S(1)} %get-tuple-element.272, f32[128,1,4]{0,2,1:T(4,128)S(1)} %get-tuple-element.269, ...), channel_id=1, replica_groups=mesh['seq'=16,'tp'=8] {'seq'}, use_global_device_ids=true, to_apply=%region_42.43 | all-reduce | flops 2048 | bytes 16384 | tf_op jit(solution)/shard_map/pmax | solution.py:163
  404.4 30.5 %all-reduce.11 = (f32[128,1,4]{0,2,1:T(4,128)S(1)}, f32[128,1,4]{0,2,1:T(4,128)S(1)}, f32[128,1,4]{0,2,1:T(4,128)S(1)}, f32[128,1,4]{0,2,1:T(4,128)S(1)}) all-reduce(f32[128,1,4]{0,2,1:T(4,128)S(1)} %get-tuple-element.741, f32[128,1,4]{0,2,1:T(4,128)S(1)} %copy-done.44, ...), channel_id=9, replica_groups=mesh['seq'=16,'tp'=8] {'seq'}, use_global_device_ids=true, to_apply=%region_45.46.clone | all-reduce | flops 2048 | bytes 16384
  436.9 48.1 %reduce-scatter.15.cloned.1.call-done = f32[8,1,4,128]{3,0,2,1:T(8,128)} async-done(((f32[128,1,4,128]{3,0,2,1:T(8,128)}), f32[8,1,4,128]{3,0,2,1:T(8,128)}) %reduce-scatter.15.cloned.1.call-update) | async-done | bytes 16400 | tf_op jit(solution)/shard_map/reduce_scatter | solution.py:167
  489.0 86.9 %all-reduce.24.cloned.1.call-done = (f32[128,1,4,128]{3,2,0,1:T(4,128)}, f32[128,1,4,128]{3,2,0,1:T(4,128)}, f32[128,1,4,128]{3,2,0,1:T(4,128)}) async-done(((f32[128,1,4,128]{3,2,0,1:T(4,128)}, f32[128,1,4,128]{3,2,0,1:T(4,128)}, f32[128,1,4,128]{3,2,0,1:T(4,128)}), (f32[128,1,4,128]{3,2,0,1:T(4,128)}, f32[128,1,4,128]{3,2,0,1:T(4,128)}, f32[128,1,4,128]{3,2,0,1:T(4,128)})) %all-reduce.24.cloned.1.call-update) | async-done | bytes 786448
  590.6 60.8 %all-reduce.28.cloned.1.call-done = (f32[8,5120]{1,0:T(8,128)}, f32[8,5120]{1,0:T(8,128)}, f32[8,5120]{1,0:T(8,128)}, f32[8,5120]{1,0:T(8,128)}) async-done(((f32[8,5120]{1,0:T(8,128)}, f32[8,5120]{1,0:T(8,128)}, f32[8,5120]{1,0:T(8,128)}, f32[8,5120]{1,0:T(8,128)}), (f32[8,5120]{1,0:T(8,128)}, f32[8,5120]{1,0:T(8,128)}, f32[8,5120]{1,0:T(8,128)}, f32[8,5120]{1,0:T(8,128)})) %all-reduce.28.cloned.1.call-update) | async-done | bytes 655376 | tf_op jit(solution)/shard_map/psum | solution.py:198
  655.9 40.9 %all-gather.5.cloned.1.call-done = bf16[128,5120]{1,0:T(8,128)(2,1)} async-done(((bf16[8,5120]{1,0:T(8,128)(2,1)}), bf16[128,5120]{1,0:T(8,128)(2,1)}) %all-gather.5.cloned.1.call-update) | async-done | bytes 1310736 | tf_op jit(solution)/shard_map/all_gather | solution.py:200
  699.4 42.6 %all-gather.7.cloned.1.call-done = bf16[128,5120]{1,0:T(8,128)(2,1)} async-done(((bf16[8,5120]{1,0:T(8,128)(2,1)}), bf16[128,5120]{1,0:T(8,128)(2,1)}) %all-gather.7.cloned.1.call-update) | async-done | bytes 1310736 | tf_op jit(solution)/shard_map/all_gather | solution.py:200
  744.6 42.0 %all-gather.9.cloned.1.call-done = bf16[128,5120]{1,0:T(8,128)(2,1)} async-done(((bf16[8,5120]{1,0:T(8,128)(2,1)}), bf16[128,5120]{1,0:T(8,128)(2,1)}) %all-gather.9.cloned.1.call-update) | async-done | bytes 1310736 | tf_op jit(solution)/shard_map/all_gather | solution.py:200
  789.3 5.2 fusion.99
  794.5 5.3 fusion.98
  799.8 5.3 fusion.97
  805.1 26.3 %all-gather.11.cloned.1.call-done = bf16[128,5120]{1,0:T(8,128)(2,1)} async-done(((bf16[8,5120]{1,0:T(8,128)(2,1)}), bf16[128,5120]{1,0:T(8,128)(2,1)}) %all-gather.11.cloned.1.call-update) | async-done | bytes 1310736 | tf_op jit(solution)/shard_map/all_gather | solution.py:200
  834.1 5.2 fusion.96
  839.4 160.1 %all-reduce.22.cloned.1.call-done = (f32[128,5120]{1,0:T(8,128)}, f32[128,5120]{1,0:T(8,128)}, f32[128,5120]{1,0:T(8,128)}, f32[128,5120]{1,0:T(8,128)}) async-done(((f32[128,5120]{1,0:T(8,128)}, f32[128,5120]{1,0:T(8,128)}, f32[128,5120]{1,0:T(8,128)}, f32[128,5120]{1,0:T(8,128)}), (f32[128,5120]{1,0:T(8,128)}, f32[128,5120]{1,0:T(8,128)}, f32[128,5120]{1,0:T(8,128)}, ...) | async-done | bytes 10485776
  1006.6 59.3 %all-reduce.26.cloned.1.call-done = (f32[8,5120]{1,0:T(8,128)}, f32[8,5120]{1,0:T(8,128)}, f32[8,5120]{1,0:T(8,128)}, f32[8,5120]{1,0:T(8,128)}) async-done(((f32[8,5120]{1,0:T(8,128)}, f32[8,5120]{1,0:T(8,128)}, f32[8,5120]{1,0:T(8,128)}, f32[8,5120]{1,0:T(8,128)}), (f32[8,5120]{1,0:T(8,128)}, f32[8,5120]{1,0:T(8,128)}, f32[8,5120]{1,0:T(8,128)}, f32[8,5120]{1,0:T(8,128)})) %all-reduce.26.cloned.1.call-update) | async-done | bytes 655376 | tf_op jit(solution)/shard_map/psum | solution.py:205
  (886 shorter events, 333.3 us)
Async XLA Ops:
  7.2 782.1 %copy-start = (bf16[256,5120]{1,0:T(8,128)(2,1)S(1)}, bf16[256,5120]{1,0:T(8,128)(2,1)}, u32[]{:S(2)}) copy-start(bf16[256,5120]{1,0:T(8,128)(2,1)} %param.33) | copy-start | bytes 7864324
  7.2 477.8 %reduce-scatter.15.cloned.1.call-start = ((), (), s32[]{:S(2)}) async-start(), calls=%async_computation.1 | async-start | bytes 278528 | tf_op jit(solution)/shard_map/reduce_scatter | solution.py:167
  26.8 75.1 %copy-start.19 = (f32[8]{0:T(128)}, f32[8]{0:T(128)S(1)}, u32[]{:S(2)}) copy-start(f32[8]{0:T(128)S(1)} %get-tuple-element.777) | copy-start | bytes 100
  123.4 48.8 %copy-start.55 = (f32[8]{0:T(128)S(1)}, f32[8]{0:T(128)}, u32[]{:S(2)}) copy-start(f32[8]{0:T(128)} %get-tuple-element.552) | copy-start | bytes 100
  123.4 48.8 %copy-start.56 = (f32[8]{0:T(128)S(1)}, f32[8]{0:T(128)}, u32[]{:S(2)}) copy-start(f32[8]{0:T(128)} %get-tuple-element.553) | copy-start | bytes 100
  172.2 91.3 %copy-start.21 = (f32[8]{0:T(128)}, f32[8]{0:T(128)S(1)}, u32[]{:S(2)}) copy-start(f32[8]{0:T(128)S(1)} %get-tuple-element.775) | copy-start | bytes 100
  285.7 99.1 %copy-start.36 = (f32[128,1,4]{0,2,1:T(4,128)S(1)}, f32[128,1,4]{0,2,1:T(4,128)}, u32[]{:S(2)}) copy-start(f32[128,1,4]{0,2,1:T(4,128)} %copy-done.35) | copy-start | bytes 6148
  285.7 100.8 %copy-start.38 = (f32[128,1,4]{0,2,1:T(4,128)S(1)}, f32[128,1,4]{0,2,1:T(4,128)}, u32[]{:S(2)}) copy-start(f32[128,1,4]{0,2,1:T(4,128)} %copy-done.37) | copy-start | bytes 6148
  355.8 31.4 %copy-start.34 = (f32[128,1,4]{0,2,1:T(4,128)}, f32[128,1,4]{0,2,1:T(4,128)S(1)}, u32[]{:S(2)}) copy-start(f32[128,1,4]{0,2,1:T(4,128)S(1)} %get-tuple-element.273) | copy-start | bytes 6148
  355.8 37.6 %copy-start.26 = (f32[8]{0:T(128)S(1)}, f32[8]{0:T(128)}, u32[]{:S(2)}) copy-start(f32[8]{0:T(128)} %copy-done.25) | copy-start | bytes 100
  355.8 39.4 %copy-start.22 = (f32[8]{0:T(128)S(1)}, f32[8]{0:T(128)}, u32[]{:S(2)}) copy-start(f32[8]{0:T(128)} %copy-done.21) | copy-start | bytes 100
  386.3 189.6 %all-reduce.24.cloned.1.call-start = ((), (), s32[]{:S(2)}) async-start(), calls=%async_computation.7 | async-start | bytes 1572864
  393.3 258.2 %all-reduce.28.cloned.1.call-start = ((), (), s32[]{:S(2)}) async-start(), calls=%async_computation.9 | async-start | bytes 1310720 | tf_op jit(solution)/shard_map/psum | solution.py:198
  400.8 34.1 %copy-start.33 = (f32[128,1,4]{0,2,1:T(4,128)S(1)}, f32[128,1,4]{0,2,1:T(4,128)}, u32[]{:S(2)}) copy-start(f32[128,1,4]{0,2,1:T(4,128)} %copy-done.32) | copy-start | bytes 6148
  400.8 34.9 %copy-start.31 = (f32[128,1,4]{0,2,1:T(4,128)S(1)}, f32[128,1,4]{0,2,1:T(4,128)}, u32[]{:S(2)}) copy-start(f32[128,1,4]{0,2,1:T(4,128)} %copy-done.30) | copy-start | bytes 6148
  400.8 35.6 %copy-start.29 = (f32[128,1,4]{0,2,1:T(4,128)S(1)}, f32[128,1,4]{0,2,1:T(4,128)}, u32[]{:S(2)}) copy-start(f32[128,1,4]{0,2,1:T(4,128)} %copy-done.28) | copy-start | bytes 6148
  400.8 36.0 %copy-start.41 = (f32[128,1,4]{0,2,1:T(4,128)S(1)}, f32[128,1,4]{0,2,1:T(4,128)}, u32[]{:S(2)}) copy-start(f32[128,1,4]{0,2,1:T(4,128)} %copy-done.40) | copy-start | bytes 6148
  586.6 66.3 %copy-start.17 = (f32[5120]{0:T(1024)S(1)}, f32[5120]{0:T(1024)}, u32[]{:S(2)}) copy-start(f32[5120]{0:T(1024)} %param.30) | copy-start | bytes 61444
  590.6 106.2 %all-gather.5.cloned.1.call-start = ((), (), s32[]{:S(2)}) async-start(), calls=%async_computation.2 | async-start | bytes 1392640 | tf_op jit(solution)/shard_map/all_gather | solution.py:200
  653.7 88.3 %all-gather.7.cloned.1.call-start = ((), (), s32[]{:S(2)}) async-start(), calls=%async_computation.3 | async-start | bytes 1392640 | tf_op jit(solution)/shard_map/all_gather | solution.py:200
  654.3 132.3 %all-gather.9.cloned.1.call-start = ((), (), s32[]{:S(2)}) async-start(), calls=%async_computation.4 | async-start | bytes 1392640 | tf_op jit(solution)/shard_map/all_gather | solution.py:200
  654.9 176.5 %all-gather.11.cloned.1.call-start = ((), (), s32[]{:S(2)}) async-start(), calls=%async_computation.5 | async-start | bytes 1392640 | tf_op jit(solution)/shard_map/all_gather | solution.py:200
  655.6 343.8 %all-reduce.22.cloned.1.call-start = ((), (), s32[]{:S(2)}) async-start(), calls=%async_computation.6 | async-start | bytes 20971520
  839.3 226.6 %all-reduce.26.cloned.1.call-start = ((), (), s32[]{:S(2)}) async-start(), calls=%async_computation.8 | async-start | bytes 1310720 | tf_op jit(solution)/shard_map/psum | solution.py:205
  (44 other events, 338.9 us)
Sparse Core Ops, SparseCore 0:
  386.4 98.5 reduce-scatter.14
  489.1 86.7 all-reduce.23
  590.7 60.6 all-reduce.27
  654.0 42.7 all-gather.4
  699.3 42.6 all-gather.6
  744.0 42.6 all-gather.8
  788.8 42.6 all-gather.10
  839.4 159.9 all-reduce.21
  1006.0 59.9 all-reduce.25
where the time goes:
time: 1080 us
  waiting for transfers between devices  569 us (53%)
  matrix products  182 us (17%)
  local copies, waits for them, and re-layouts  138 us (13%)
  blocking collectives  131 us (12%)
  other arithmetic  39.5 us (4%)
  between operations  16.3 us (2%)
    unnamed x11, waiting for transfers between devices  249 us
    all_gather x4, waiting for transfers between devices, local(): row_piece = lax.all_gather(normed_mlp, 'seq', axis=0, tiled=True)  152 us
    all_gather x4, blocking collectives, local(): all_queries = lax.all_gather(query_head_rows, 'seq', axis=0, tiled=True)  71.1 us
    psum x1, waiting for transfers between devices, local(): lax.psum(head_part, 'tp')  60.8 us
    psum x1, waiting for transfers between devices, local(): summed_units = lax.psum(partial_terms, 'tp')  59.3 us
    reduce_scatter x1, waiting for transfers between devices, local(): lax.psum_scatter(local_acc * factor[..., None], 'seq', scatter_dimension=...  48.1 us
    dot_general x36, matrix products, block_step(): jnp.einsum('pkgd,pktd->pkgt', page_query, keys_block, preferred_element_t...  43.5 us
    dot_general x36, matrix products, block_step(): jnp.einsum('pkgt,pktd->pkgd', weights.astype(jnp.bfloat16), values_block,...  41.6 us
  transfers between devices with their start and end apart: 9, of which 9 were waited for; matrix products, arithmetic and copies ran while one was open for 4% of the time, Pallas kernels for 0%

commit v1 on v0

v1 whole, which is shorter than its diff:
```python
import functools

import jax
import jax.numpy as jnp
from jax import lax
from jax.experimental import pallas as pl
from jax.experimental.pallas import tpu as pltpu
from jax.sharding import PartitionSpec as P

STEPS = 4
rope_theta = 100000000.0
norm_eps = 1e-05
masked_low = -1e30


def rms_norm(values, gain):
    floats = values.astype(jnp.float32)
    square_mean = jnp.mean(floats * floats, axis=-1, keepdims=True)
    return floats * lax.rsqrt(square_mean + norm_eps) * gain


def rotary_tables(token_position, head_dim):
    half_dim = head_dim // 2
    exponent = jnp.arange(half_dim, dtype=jnp.float32) * (2.0 / head_dim)
    inverse_freq = rope_theta ** (-exponent)
    angles = token_position.astype(jnp.float32)[:, None] * inverse_freq[None, :]
    return jnp.cos(angles), jnp.sin(angles)


def rotate(values, cosine, sine):
    half = values.shape[-1] // 2
    a = values[..., :half]
    b = values[..., half:]
    return jnp.concatenate([a * cosine - b * sine, b * cosine + a * sine], axis=-1)


def paged_kernel(pages, rows_ref, valid_ref, q_ref, k_ref, v_ref, o_ref, lse_ref, m_s, l_s, acc_s):
    step = pl.program_id(0)
    scale = k_ref.shape[-1] ** (-0.5)

    @pl.when(step == 0)
    def _():
        m_s[...] = jnp.full_like(m_s, masked_low)
        l_s[...] = jnp.zeros_like(l_s)
        acc_s[...] = jnp.zeros_like(acc_s)

    stats = []
    for i in range(pages):
        page = step * pages + i
        row = rows_ref[page]
        valid = valid_ref[page]
        q = q_ref[row]
        s = (
            lax.dot_general(
                q, k_ref[i], (((1,), (1,)), ((), ())), preferred_element_type=jnp.float32
            )
            * scale
        )
        live = lax.broadcasted_iota(jnp.int32, s.shape, 1) < valid
        s = jnp.where(live, s, masked_low)
        m = jnp.max(s, axis=-1, keepdims=True)
        w = jnp.where(live, jnp.exp(s - m), 0.0)
        l = jnp.sum(w, axis=-1, keepdims=True)
        acc = jnp.dot(w.astype(jnp.bfloat16), v_ref[i], preferred_element_type=jnp.float32)
        stats.append((row, m, l, acc))
    for row, m, l, acc in stats:
        m_old = m_s[row]
        m_new = jnp.maximum(m_old, m)
        a_old = jnp.exp(m_old - m_new)
        a_new = jnp.exp(m - m_new)
        m_s[row] = m_new
        l_s[row] = l_s[row] * a_old + l * a_new
        acc_s[row] = acc_s[row] * a_old + acc * a_new

    @pl.when(step == pl.num_programs(0) - 1)
    def _():
        l = l_s[...]
        safe = jnp.where(l > 0.0, l, 1.0)
        o_ref[...] = (acc_s[...] / safe).astype(o_ref.dtype)
        lse = jnp.where(l > 0.0, m_s[...] + jnp.log(safe), masked_low)
        eye = lax.broadcasted_iota(jnp.int32, lse.shape, 1) == lax.broadcasted_iota(
            jnp.int32, lse.shape, 2
        )
        lse_ref[...] = jnp.sum(jnp.where(eye, lse, 0.0), axis=1)


def paged_attention(rows, valid, queries, keys, values):
    total, group, dim = queries.shape
    count, length, _ = keys.shape
    pages = next(n for n in (6, 4, 3, 2, 1) if count % n == 0)
    return pl.pallas_call(
        functools.partial(paged_kernel, pages),
        grid_spec=pltpu.PrefetchScalarGridSpec(
            num_scalar_prefetch=2,
            grid=(count // pages,),
            in_specs=[
                pl.BlockSpec((total, group, dim), lambda i, *_: (0, 0, 0)),
                pl.BlockSpec((pages, length, dim), lambda i, *_: (i, 0, 0)),
                pl.BlockSpec((pages, length, dim), lambda i, *_: (i, 0, 0)),
            ],
            out_specs=[
                pl.BlockSpec((total, group, dim), lambda i, *_: (0, 0, 0)),
                pl.BlockSpec((total, dim), lambda i, *_: (0, 0)),
            ],
            scratch_shapes=[
                pltpu.VMEM((total, group, dim), jnp.float32),
                pltpu.VMEM((total, group, dim), jnp.float32),
                pltpu.VMEM((total, group, dim), jnp.float32),
            ],
        ),
        out_shape=[
            jax.ShapeDtypeStruct((total, group, dim), jnp.bfloat16),
            jax.ShapeDtypeStruct((total, dim), jnp.float32),
        ],
        name="paged_attention",
    )(rows, valid, queries, keys, values)


def local(
    token_inputs,
    attn_gain,
    w_query,
    key_projection,
    value_projection,
    w_output,
    mlp_gain,
    w_gate,
    w_up,
    w_down,
    key_cache,
    paged_value_cache,
    cache_lengths,
    page_request,
    page_number,
    request_slot,
):
    steps, row_count, width = token_inputs.shape
    seq = lax.axis_size("seq")
    total_rows = row_count * seq
    page_count, kv_local, page_size, head_dim = key_cache.shape
    group = w_query.shape[1] // head_dim
    scale = head_dim ** (-0.5)
    first_row = lax.axis_index("seq") * row_count
    own_rows = first_row + jnp.arange(row_count, dtype=jnp.int32)
    own_match = request_slot[None, :] == own_rows[:, None]
    row_lengths = jnp.sum(jnp.where(own_match, cache_lengths[None, :], 0), axis=1)
    page_live = page_request >= 0
    page_req = jnp.where(page_live, page_request, 0)
    req_match = page_req[:, None] == jnp.arange(total_rows, dtype=jnp.int32)[None, :]
    page_row = jnp.sum(jnp.where(req_match, request_slot[None, :], 0), axis=1)
    page_len = jnp.sum(jnp.where(req_match, cache_lengths[None, :], 0), axis=1)
    valid = jnp.where(page_live, jnp.clip(page_len - page_number * page_size, 0, page_size), 0)

    x = token_inputs.reshape(steps * row_count, width)
    normed = rms_norm(x, attn_gain).astype(jnp.bfloat16)
    position = (jnp.arange(steps, dtype=jnp.int32)[:, None] + row_lengths[None, :]).reshape(-1)
    cosine, sine = rotary_tables(position, head_dim)
    q = jnp.dot(normed, w_query, preferred_element_type=jnp.float32)
    q = rotate(q.reshape(-1, group, head_dim), cosine[:, None], sine[:, None])
    q = q.astype(jnp.bfloat16).reshape(steps, row_count, group, head_dim)
    fresh_k = rotate(
        jnp.dot(normed, key_projection, preferred_element_type=jnp.float32), cosine, sine
    )
    fresh_k = fresh_k.astype(jnp.bfloat16).reshape(steps, row_count, head_dim)
    fresh_v = jnp.dot(normed, value_projection, preferred_element_type=jnp.float32)
    fresh_v = fresh_v.astype(jnp.bfloat16).reshape(steps, row_count, head_dim)
    q = jnp.swapaxes(q, 0, 1).reshape(row_count, steps * group, head_dim)
    all_q = lax.all_gather(q, "seq", axis=0, tiled=True)
    part, lse = paged_attention(
        page_row, valid, all_q, key_cache[:, 0], paged_value_cache[:, 0]
    )
    part = lax.all_to_all(part.reshape(seq, row_count, steps * group, head_dim), "seq", 0, 0)
    lse = lax.all_to_all(lse.reshape(seq, row_count, head_dim), "seq", 0, 0)
    lse = lse[:, :, : steps * group]
    s = jnp.einsum("rqd,jrd->rqj", q, fresh_k, preferred_element_type=jnp.float32) * scale
    allowed = (
        jnp.arange(steps)[None, :] <= (jnp.arange(steps * group) // group)[:, None]
    )
    s = jnp.where(allowed[None], s, masked_low)
    recent_max = jnp.max(s, axis=-1)
    w = jnp.where(allowed[None], jnp.exp(s - recent_max[..., None]), 0.0)
    recent_sum = jnp.sum(w, axis=-1)
    recent_acc = jnp.einsum(
        "rqj,jrd->rqd", w.astype(jnp.bfloat16), fresh_v, preferred_element_type=jnp.float32
    )
    top = jnp.maximum(jnp.max(lse, axis=0), recent_max)
    factor = jnp.exp(lse - top[None])
    fresh_factor = jnp.exp(recent_max - top)
    total = jnp.sum(factor, axis=0) + recent_sum * fresh_factor
    acc = jnp.sum(part.astype(jnp.float32) * factor[..., None], axis=0)
    acc = acc + recent_acc * fresh_factor[..., None]
    attention = (acc / total[..., None]).astype(jnp.bfloat16)
    attention = jnp.swapaxes(attention.reshape(row_count, steps, group * head_dim), 0, 1)
    attention = attention.reshape(steps * row_count, group * head_dim)
    head_part = jnp.dot(attention, w_output, preferred_element_type=jnp.float32)
    attended = (x.astype(jnp.float32) + lax.psum(head_part, "tp")).astype(jnp.bfloat16)
    normed_mlp = rms_norm(attended, mlp_gain).astype(jnp.bfloat16)
    everyone = lax.all_gather(normed_mlp, "seq", axis=0, tiled=True)
    gate = jnp.dot(everyone, w_gate, preferred_element_type=jnp.float32)
    up = jnp.dot(everyone, w_up, preferred_element_type=jnp.float32)
    activation = (jax.nn.silu(gate) * up).astype(jnp.bfloat16)
    partial = jnp.dot(activation, w_down, preferred_element_type=jnp.float32)
    mlp = lax.psum_scatter(partial, "seq", scatter_dimension=0, tiled=True)
    mlp = lax.psum(mlp, "tp")
    layer_out = (attended.astype(jnp.float32) + mlp).astype(jnp.bfloat16)
    shape = (steps, row_count, width)
    return attended.reshape(shape), layer_out.reshape(shape)


def solution(mesh):
    in_specs = (
        P(None, "seq", None),
        P(),
        P(None, "tp"),
        P(None, "tp"),
        P(None, "tp"),
        P("tp", None),
        P(),
        P(None, ("seq", "tp")),
        P(None, ("seq", "tp")),
        P(("seq", "tp"), None),
        P("seq", "tp", None, None),
        P("seq", "tp", None, None),
        P(),
        P("seq"),
        P("seq"),
        P(),
    )
    out_specs = (P(None, "seq", None), P(None, "seq", None))
    return jax.shard_map(local, mesh=mesh, in_specs=in_specs, out_specs=out_specs, check_vma=False)
```

time: 1080 us -> 396 us (0.37)
  waiting for transfers between devices: 569 us -> 287 us
  matrix products: 182 us -> 30.3 us
  local copies, waits for them, and re-layouts: 138 us -> 8.16 us
  blocking collectives: 131 us -> 22.8 us
  other arithmetic: 39.5 us -> 11 us
  Pallas kernels: 0 us -> 12.8 us
    unnamed x11 -> x4, waiting for transfers between devices: 249 us -> 0.07 us
    dot_general x171 -> x7, matrix products: 166 us -> 25.9 us  [the longest x1 12.9 us: local(): partial = jnp.dot(activation, w_down, preferred_element_type=jnp.float32)]
    all_gather x4 -> x1, waiting for transfers between devices: 152 us -> 57.9 us  [local(): everyone = lax.all_gather(normed_mlp, 'seq', axis=0, tiled=True)]
    gather x76 -> x0, local copies, waits for them, and re-layouts: 77.2 us -> none  [the longest x36 37.2 us: block_step(): page_query = all_queries[rows_block]]
    all_gather x4 -> x1, blocking collectives: 71.1 us -> 22.8 us  [local(): all_q = lax.all_gather(q, 'seq', axis=0, tiled=True)]
    reduce_scatter x1, waiting for transfers between devices: 48.1 us -> 89 us  [local(): mlp = lax.psum_scatter(partial, 'seq', scatter_dimension=0, tiled=True)]
    unnamed x1 -> x0, blocking collectives: 30.5 us -> none
    pmax x1 -> x0, blocking collectives: 29 us -> none  [local(): global_max = lax.pmax(local_max, 'seq')]
  transfers between devices with their start and end apart: 9 -> 6, of which waited for: 9 -> 6; matrix products, arithmetic and copies ran while one was open for 4% -> 1% of each run, Pallas kernels for 0% -> 0%
where the time goes in v1:
time: 396 us; the launch traced here: 394 us
  waiting for transfers between devices  287 us (72%)
  matrix products  30.3 us (8%)
  blocking collectives  22.8 us (6%)
  between operations  14 us (4%)
  Pallas kernels  12.8 us (3%)
  other arithmetic  11 us (3%)
  starting transfers between devices  8.36 us (2%)
  local copies, waits for them, and re-layouts  8.16 us (2%)
    reduce_scatter x1, waiting for transfers between devices, local(): mlp = lax.psum_scatter(partial, 'seq', scatter_dimension=0, tiled=True)  89 us
    psum x1, waiting for transfers between devices, local(): lax.psum(head_part, 'tp')  65 us
    psum x1, waiting for transfers between devices, local(): mlp = lax.psum(mlp, 'tp')  61.9 us
    all_gather x1, waiting for transfers between devices, local(): everyone = lax.all_gather(normed_mlp, 'seq', axis=0, tiled=True)  57.9 us
    all_gather x1, blocking collectives, local(): all_q = lax.all_gather(q, 'seq', axis=0, tiled=True)  22.8 us
    dot_general x1, matrix products, local(): partial = jnp.dot(activation, w_down, preferred_element_type=jnp.float32)  12.9 us
    pallas_call x1, Pallas kernels, paged_attention(): pl.pallas_call(functools.partial(paged_kernel, pages), grid_spec=pltpu.Pr...  12.8 us
    all_to_all x1, waiting for transfers between devices, local(): lax.all_to_all(part.reshape(seq, row_count, steps * group, head_dim), 'se...  8.21 us
  transfers between devices with their start and end apart: 6, of which 6 were waited for; matrix products, arithmetic and copies ran while one was open for 1% of the time, Pallas kernels for 0%

profile of v1, /device:TPU:1, one launch (start us, length us, event | category | flops | bytes accessed | tf_op | source)
XLA Modules:
  0.0 394.0 jit_solution(8981392117692876997)
XLA Ops:
  8.0 0.9 select_reduce_fusion.2
  8.9 1.4 select_reduce_fusion
  10.3 1.1 fusion.16
  11.6 7.9 %copy.43 = bf16[512,5120]{1,0:T(8,128)(2,1)} copy(bf16[512,5120]{0,1:T(8,128)(2,1)} %bitcast.58) | data formatting | bytes 10485760 | tf_op jit(solution)/shard_map/dot_general | solution.py:158
  19.5 4.2 %fusion.25 = f32[32,4,128]{2,0,1:T(8,128)S(1)} fusion(bf16[4,128,5120]{2,1,0:T(8,128)(2,1)} %bitcast.57, bf16[4,8,5120]{2,1,0:T(8,128)(2,1)S(1)} %copy-done.1, f32[5120]{0:T(1024)S(1)} %copy-done.4, f32[4,8]{1,0:T(4,128)S(1)} %add_rsqrt_fusion), kind=kOutput, calls=%fused_computation.36 | convolution fusion | flops 168427520 | bytes 5656704 | tf_op jit(solution)/shard_map/dot_general | solution.py:158
  24.5 22.8 %all_gather.6.q_ref = bf16[128,16,128]{2,1,0:T(8,128)(2,1)} all-gather(bf16[8,16,128]{2,1,0:T(8,128)(2,1)S(1)} %bitcast.63), channel_id=1, replica_groups=mesh['seq'=16,'tp'=8] {'seq'}, dimensions={0}, use_global_device_ids=true | all-gather | bytes 557056 | tf_op jit(solution)/shard_map/all_gather | solution.py:168
  47.9 12.8 %paged_attention.1 = (bf16[128,16,128]{2,1,0:T(8,128)(2,1)}, f32[128,128]{1,0:T(8,128)}) custom-call(s32[36]{0:T(128)} %get-tuple-element.7.rows_ref, s32[36]{0:T(128)} %compare_select_fusion.valid_ref, bf16[128,16,128]{2,1,0:T(8,128)(2,1)} %all_gather.6.q_ref, bf16[36,256,128]{2,1,0:T(8,128)(2,1)} %bitcast.60, bf16[36,256,128]{2,1,0:T(8,128)(2,1)} %bitcast.61), custom_call_target="tpu_custom_call" | custom-call | tf_op jit(solution)/shard_map/paged_attention/pallas_call | solution.py:91
  60.7 4.6 %all-to-all-start.1 = ((f32[16,8,128]{2,1,0:T(8,128)}), f32[16,8,128]{2,1,0:T(8,128)S(1)}, u32[]{:S(2)}, u32[]{:S(2)}) async-start(f32[16,8,128]{2,1,0:T(8,128)} %bitcast.65), calls=%async_computation.1 | async-start | bytes 131072 | tf_op jit(solution)/shard_map/all_to_all | solution.py:173
  65.3 1.7 fusion.6
  67.3 4.5 %all-to-all-done.1 = f32[16,8,128]{2,1,0:T(8,128)S(1)} async-done(((f32[16,8,128]{2,1,0:T(8,128)}), f32[16,8,128]{2,1,0:T(8,128)S(1)}, u32[]{:S(2)}, u32[]{:S(2)}) %all-to-all-start.1) | async-done | bytes 65568 | tf_op jit(solution)/shard_map/all_to_all | solution.py:173
  71.8 3.6 all-to-all-start
  76.1 8.2 %all-to-all-done = bf16[16,8,16,128]{3,2,1,0:T(8,128)(2,1)S(1)} async-done(((bf16[16,8,16,128]{3,2,1,0:T(8,128)(2,1)}), bf16[16,8,16,128]{3,2,1,0:T(8,128)(2,1)S(1)}, u32[]{:S(2)}, u32[]{:S(2)}) %all-to-all-start) | async-done | bytes 524320 | tf_op jit(solution)/shard_map/all_to_all | solution.py:172
  84.4 1.2 multiply_reduce_fusion
  85.5 0.9 fusion.4
  86.5 4.4 %fusion.36 = f32[32,5120]{1,0:T(8,128)} fusion(bf16[512,5120]{1,0:T(8,128)(2,1)} %param.21, bf16[8,4,512]{2,1,0:T(4,128)(2,1)S(1)} %reshape.217), kind=kOutput, calls=%fused_computation.49 | convolution fusion | flops 167772160 | bytes 5931008 | tf_op jit(solution)/shard_map/dot_general | solution.py:195
  90.9 65.0 %all-reduce.3.cloned.1.call-done = f32[32,5120]{1,0:T(8,128)} async-done(((f32[32,5120]{1,0:T(8,128)}), f32[32,5120]{1,0:T(8,128)}) %all-reduce.3.cloned.1.call-update) | async-done | bytes 655376 | tf_op jit(solution)/shard_map/psum | solution.py:196
  155.9 1.3 fusion.12
  157.3 0.9 fusion.14
  158.2 57.9 %all-gather.2.cloned.1.call-done = bf16[512,5120]{1,0:T(8,128)(2,1)} async-done(((bf16[32,5120]{1,0:T(8,128)(2,1)}), bf16[512,5120]{1,0:T(8,128)(2,1)}) %all-gather.2.cloned.1.call-update) | async-done | bytes 5242896 | tf_op jit(solution)/shard_map/all_gather | solution.py:198
  216.1 5.6 %fusion.57 = f32[512,256]{1,0:T(8,128)} fusion(bf16[512,5120]{1,0:T(8,128)(2,1)} %all-gather.2.cloned.1.call-done, bf16[5120,256]{1,0:T(8,128)(2,1)} %param.23), kind=kOutput, calls=%fused_computation.91 | convolution fusion | flops 1342177280 | bytes 8388608 | tf_op jit(solution)/shard_map/dot_general | solution.py:199
  221.8 12.9 %fusion.1 = f32[512,5120]{1,0:T(8,128)} fusion(bf16[256,5120]{1,0:T(8,128)(2,1)S(1)} %copy-done, bf16[512,5120]{1,0:T(8,128)(2,1)} %all-gather.2.cloned.1.call-done, bf16[5120,256]{1,0:T(8,128)(2,1)} %param.24, f32[512,256]{1,0:T(8,128)} %fusion.57), kind=kOutput, calls=%fused_computation.2 | convolution fusion | flops 2685140992 | bytes 21495808 | tf_op jit(solution)/shard_map/dot_general | solution.py:202
  234.7 89.0 %reduce-scatter.2.cloned.1.call-done = f32[32,5120]{1,0:T(8,128)} async-done(((f32[512,5120]{1,0:T(8,128)}), f32[32,5120]{1,0:T(8,128)}) %reduce-scatter.2.cloned.1.call-update) | async-done | bytes 655376 | tf_op jit(solution)/shard_map/reduce_scatter | solution.py:203
  323.8 61.9 %all-reduce.5.cloned.1.call-done = f32[32,5120]{1,0:T(8,128)} async-done(((f32[32,5120]{1,0:T(8,128)}), f32[32,5120]{1,0:T(8,128)}) %all-reduce.5.cloned.1.call-update) | async-done | bytes 655376 | tf_op jit(solution)/shard_map/psum | solution.py:204
  385.6 1.9 fusion.27
  (53 shorter events, 3.6 us)
Async XLA Ops:
  7.2 214.6 %copy-start = (bf16[256,5120]{1,0:T(8,128)(2,1)S(1)}, bf16[256,5120]{1,0:T(8,128)(2,1)}, u32[]{:S(2)}) copy-start(bf16[256,5120]{1,0:T(8,128)(2,1)} %param.25) | copy-start | bytes 7864324
  11.6 7.9 %copy-start.1 = (bf16[4,8,5120]{2,1,0:T(8,128)(2,1)S(1)}, bf16[4,8,5120]{2,1,0:T(8,128)(2,1)}, u32[]{:S(2)}) copy-start(bf16[4,8,5120]{2,1,0:T(8,128)(2,1)} %param.16) | copy-start | bytes 983044
  11.6 7.9 %copy-start.4 = (f32[5120]{0:T(1024)S(1)}, f32[5120]{0:T(1024)}, u32[]{:S(2)}) copy-start(f32[5120]{0:T(1024)} %param.17) | copy-start | bytes 61444
  19.5 4.3 %copy-start.3 = (bf16[5120,128]{1,0:T(8,128)(2,1)S(1)}, bf16[5120,128]{1,0:T(8,128)(2,1)}, u32[]{:S(2)}) copy-start(bf16[5120,128]{1,0:T(8,128)(2,1)} %param.19) | copy-start | bytes 3932164
  23.7 23.6 %copy-start.8 = (s32[36]{0:T(128)S(1)}, s32[36]{0:T(128)}, u32[]{:S(2)}) copy-start(s32[36]{0:T(128)} %param.29) | copy-start | bytes 436
  23.7 23.6 %copy-start.9 = (s32[36]{0:T(128)S(1)}, s32[36]{0:T(128)}, u32[]{:S(2)}) copy-start(s32[36]{0:T(128)} %param.30) | copy-start | bytes 436
  60.7 11.1 %all-to-all-start.1 = ((f32[16,8,128]{2,1,0:T(8,128)}), f32[16,8,128]{2,1,0:T(8,128)S(1)}, u32[]{:S(2)}, u32[]{:S(2)}) async-start(f32[16,8,128]{2,1,0:T(8,128)} %bitcast.65), calls=%async_computation.1 | async-start | bytes 131072 | tf_op jit(solution)/shard_map/all_to_all | solution.py:173
  65.3 6.5 %copy-start.7 = (pred[16,4]{0,1:T(4,128)(4,1)}, pred[16,4]{0,1:T(4,128)(4,1)S(1)}, u32[]{:S(2)}) copy-start(pred[16,4]{0,1:T(4,128)(4,1)S(1)} %iota_compare_fusion.1) | copy-start | bytes 196
  67.3 4.6 %copy-start.6 = (f32[8,16,4]{1,2,0:T(4,128)}, f32[8,16,4]{1,2,0:T(4,128)S(1)}, u32[]{:S(2)}) copy-start(f32[8,16,4]{1,2,0:T(4,128)S(1)} %get-tuple-element.21) | copy-start | bytes 6148
  71.8 12.5 %all-to-all-start = ((bf16[16,8,16,128]{3,2,1,0:T(8,128)(2,1)}), bf16[16,8,16,128]{3,2,1,0:T(8,128)(2,1)S(1)}, u32[]{:S(2)}, u32[]{:S(2)}) async-start(bf16[16,8,16,128]{3,2,1,0:T(8,128)(2,1)} %bitcast.62), calls=%async_computation | async-start | bytes 1048576 | tf_op jit(solution)/shard_map/all_to_all | solution.py:172
  75.4 80.5 %all-reduce.3.cloned.1.call-start = ((), (), s32[]{:S(2)}) async-start(), calls=%async_computation.3 | async-start | bytes 1310720 | tf_op jit(solution)/shard_map/psum | solution.py:196
  86.5 70.7 %copy-start.5 = (f32[5120]{0:T(1024)S(1)}, f32[5120]{0:T(1024)}, u32[]{:S(2)}) copy-start(f32[5120]{0:T(1024)} %param.22) | copy-start | bytes 61444
  90.9 125.2 %all-gather.2.cloned.1.call-start = ((), (), s32[]{:S(2)}) async-start(), calls=%async_computation.4 | async-start | bytes 5570560 | tf_op jit(solution)/shard_map/all_gather | solution.py:198
  157.2 228.4 %copy-start.2 = (bf16[32,5120]{1,0:T(8,128)(2,1)}, bf16[32,5120]{1,0:T(8,128)(2,1)S(1)}, u32[]{:S(2)}) copy-start(bf16[32,5120]{1,0:T(8,128)(2,1)S(1)} %get-tuple-element.9) | copy-start | bytes 983044
  158.1 165.6 %reduce-scatter.2.cloned.1.call-start = ((), (), s32[]{:S(2)}) async-start(), calls=%async_computation.5 | async-start | bytes 11141120 | tf_op jit(solution)/shard_map/reduce_scatter | solution.py:203
  234.7 151.0 %all-reduce.5.cloned.1.call-start = ((), (), s32[]{:S(2)}) async-start(), calls=%async_computation.6 | async-start | bytes 1310720 | tf_op jit(solution)/shard_map/psum | solution.py:204
Sparse Core Ops, SparseCore 0:
  91.0 64.8 all-reduce.2
  158.6 57.4 all-gather.1
  234.8 88.9 reduce-scatter.1
  325.9 59.6 all-reduce.4

commit v2 on v1

--- a/solution.py
+++ b/solution.py
@@ -114,6 +114,572 @@
         ],
         name="paged_attention",
     )(rows, valid, queries, keys, values)
+
+
+AXES = (("y", "x", "z"), ("x", "z", "y"), ("z", "y", "x"))
+MESH = pl.DeviceIdType.MESH
+
+
+class Place:
+    def __init__(self):
+        s = lax.axis_index("seq")
+        t = lax.axis_index("tp")
+        self.at = {"z": s // 4, "x": s % 4, "y": t // 2}
+        self.core = t % 2
+        self.s = s
+        self.t = t
+
+    def shifted(self, axis, by):
+        return lax.rem(self.at[axis] + (by + 4), 4)
+
+    def device(self, axis=None, by=0, flip=False):
+        at = dict(self.at)
+        if axis is not None:
+            at[axis] = self.shifted(axis, by)
+        core = 1 - self.core if flip else self.core
+        return {"seq": at["z"] * 4 + at["x"], "tp": at["y"] * 2 + core}
+
+
+class Wire:
+    def __init__(self, send_sem, recv_sem):
+        self.send_sem = send_sem
+        self.recv_sem = recv_sem
+        self.used = 0
+        self.sent = []
+
+    def slot(self):
+        self.used += 1
+        return self.used - 1
+
+    def send(self, slot, src, dst, device):
+        copy = pltpu.make_async_remote_copy(
+            src_ref=src,
+            dst_ref=dst,
+            send_sem=self.send_sem.at[slot],
+            recv_sem=self.recv_sem.at[slot],
+            device_id=device,
+            device_id_type=MESH,
+        )
+        copy.start()
+        self.sent.append(copy)
+
+    def recv(self, slot, dst, device):
+        pltpu.make_async_remote_copy(
+            src_ref=dst,
+            dst_ref=dst,
+            send_sem=self.send_sem.at[slot],
+            recv_sem=self.recv_sem.at[slot],
+            device_id=device,
+            device_id_type=MESH,
+        ).wait_recv()
+
+    def drain(self):
+        for copy in self.sent:
+            copy.wait_send()
+
+
+def greet(place):
+    barrier = pltpu.get_barrier_semaphore()
+    peers = [{"seq": place.s, "tp": lax.rem(place.t + j, 8)} for j in range(1, 8)]
+    peers += [place.device(axis, by) for axis in ("x", "z") for by in (1, 2, 3)]
+    for peer in peers:
+        pl.semaphore_signal(barrier, inc=1, device_id=peer, device_id_type=MESH)
+    return barrier, len(peers)
+
+
+class Gather:
+    def __init__(self, wire, place, axes, buf):
+        self.wire, self.place, self.buf = wire, place, buf
+        self.a, self.b, self.c = axes
+        self.slots_a = [wire.slot() for _ in range(3)]
+        self.slots_b = [wire.slot() for _ in range(4)]
+        self.slots_c = [[wire.slot() for _ in range(4)] for _ in range(4)]
+        self.slots_p = [[wire.slot() for _ in range(4)] for _ in range(4)]
+
+    def group(self, db, dc, core=None):
+        place = self.place
+        core = place.core if core is None else core
+        return self.buf.at[core, place.shifted(self.c, dc), place.shifted(self.b, db)]
+
+    def half(self, db, dc, which):
+        place = self.place
+        return self.buf.at[
+            place.core, place.shifted(self.c, dc), place.shifted(self.b, db), pl.ds(2 * which, 2)
+        ]
+
+    def block(self, da):
+        place = self.place
+        return self.buf.at[
+            place.core, place.at[self.c], place.at[self.b], place.shifted(self.a, da)
+        ]
+
+    def open(self):
+        mine = self.block(0)
+        for j in (2, 1, 3):
+            self.wire.send(self.slots_a[j - 1], mine, mine, self.place.device(self.a, j))
+
+    def spread(self, db):
+        mine = self.group(db, 0)
+        slots = self.slots_c[db]
+        self.wire.send(slots[0], mine, mine, self.place.device(self.c, 1))
+        self.wire.send(slots[1], mine, mine, self.place.device(self.c, -1))
+        self.over(db, 0)
+
+    def over(self, db, dc):
+        mine = self.group(db, dc)
+        self.wire.send(self.slots_p[db][dc], mine, mine, self.place.device(flip=True))
+
+    def line(self):
+        for j in (1, 3, 2):
+            self.wire.recv(self.slots_a[j - 1], self.block(-j), self.place.device(self.a, -j))
+        mine = self.group(0, 0)
+        self.wire.send(self.slots_b[0], mine, mine, self.place.device(self.b, 1))
+        self.wire.send(self.slots_b[1], mine, mine, self.place.device(self.b, -1))
+        self.spread(0)
+
+    def plane_near(self):
+        place, wire = self.place, self.wire
+        wire.recv(self.slots_b[0], self.group(-1, 0), place.device(self.b, -1))
+        part = self.half(-1, 0, 0)
+        wire.send(self.slots_b[2], part, part, place.device(self.b, 1))
+        wire.recv(self.slots_b[1], self.group(1, 0), place.device(self.b, 1))
+        part = self.half(1, 0, 1)
+        wire.send(self.slots_b[3], part, part, place.device(self.b, -1))
+        self.spread(3)
+        self.spread(1)
+
+    def plane_far(self):
+        place, wire = self.place, self.wire
+        wire.recv(self.slots_b[2], self.half(2, 0, 0), place.device(self.b, -1))
+        wire.recv(self.slots_b[3], self.half(2, 0, 1), place.device(self.b, 1))
+        self.spread(2)
+
+    def space_near(self, db):
+        place, wire = self.place, self.wire
+        slots = self.slots_c[db]
+        wire.recv(slots[0], self.group(db, -1), place.device(self.c, -1))
+        part = self.half(db, -1, 0)
+        wire.send(slots[2], part, part, place.device(self.c, 1))
+        wire.recv(slots[1], self.group(db, 1), place.device(self.c, 1))
+        part = self.half(db, 1, 1)
+        wire.send(slots[3], part, part, place.device(self.c, -1))
+        self.over(db, 3)
+        self.over(db, 1)
+
+    def space_far(self, db):
+        place, wire = self.place, self.wire
+        slots = self.slots_c[db]
+        wire.recv(slots[2], self.half(db, 2, 0), place.device(self.c, -1))
+        wire.recv(slots[3], self.half(db, 2, 1), place.device(self.c, 1))
+        self.over(db, 2)
+
+    def other_core(self):
+        place = self.place
+        for db in (0, 3, 1, 2):
+            for dc in (0, 3, 1, 2):
+                self.wire.recv(
+                    self.slots_p[db][dc],
+                    self.group(db, dc, 1 - place.core),
+                    place.device(flip=True),
+                )
+
+
+def add_into(dst, src, count):
+    def body(i, carry):
+        total = dst[i].astype(jnp.float32) + src[i].astype(jnp.float32)
+        dst[i] = total.astype(dst.dtype)
+        return carry
+
+    lax.fori_loop(0, count, body, 0)
+
+
+class Scatter:
+    def __init__(self, wire, place, axis, piece, relay, near):
+        self.wire, self.place, self.axis = wire, place, axis
+        self.piece, self.relay, self.near = piece, relay, near
+        self.slots = [wire.slot() for _ in range(6)]
+
+    def open(self):
+        w, p = self.wire, self.place
+        up, down = p.device(self.axis, 1), p.device(self.axis, -1)
+        w.send(self.slots[0], self.piece(2, 0), self.relay.at[0], up)
+        w.send(self.slots[1], self.piece(2, 1), self.relay.at[1], down)
+        w.send(self.slots[2], self.piece(1, 1), self.near.at[0, 1], up)
+        w.send(self.slots[3], self.piece(-1, 0), self.near.at[1, 0], down)
+
+    def pass_on(self, count):
+        w, p = self.wire, self.place
+        up, down = p.device(self.axis, 1), p.device(self.axis, -1)
+        w.recv(self.slots[0], self.relay.at[0], down)
+        add_into(self.piece(1, 0), self.relay.at[0], count)
+        w.send(self.slots[4], self.piece(1, 0), self.near.at[0, 0], up)
+        w.recv(self.slots[1], self.relay.at[1], up)
+        add_into(self.piece(-1, 1), self.relay.at[1], count)
+        w.send(self.slots[5], self.piece(-1, 1), self.near.at[1, 1], down)
+
+    def close(self):
+        w, p = self.wire, self.place
+        up, down = p.device(self.axis, 1), p.device(self.axis, -1)
+        w.recv(self.slots[2], self.near.at[0, 1], down)
+        w.recv(self.slots[3], self.near.at[1, 0], up)
+        w.recv(self.slots[4], self.near.at[0, 0], down)
+        w.recv(self.slots[5], self.near.at[1, 1], up)
+
+
+def slots_needed():
+    class Count:
+        def __init__(self):
+            self.n = 0
+
+        def slot(self):
+            self.n += 1
+            return self.n - 1
+
+    return 7 + 3 * (3 + 4 + 16 + 16) + 12 + 3 * (6 + 6 + 3) + 7
+
+
+def block_kernel(
+    widths,
+    att_ref,
+    x_ref,
+    wo_hbm,
+    wgu_hbm,
+    wd_hbm,
+    attended_ref,
+    layer_ref,
+    wo,
+    wgu,
+    wd,
+    s1,
+    r1,
+    g0,
+    g1,
+    g2,
+    acc,
+    squares,
+    act,
+    p0,
+    p1,
+    p2,
+    o0,
+    o1,
+    o2,
+    rc0,
+    rc1,
+    rc2,
+    nc0,
+    nc1,
+    nc2,
+    q0,
+    q1,
+    q2,
+    rb0,
+    rb1,
+    rb2,
+    nb0,
+    nb1,
+    nb2,
+    ta0,
+    ta1,
+    ta2,
+    ra0,
+    ra1,
+    ra2,
+    mine_s,
+    last,
+    load_sem,
+    send_sem,
+    recv_sem,
+):
+    place = Place()
+    t, core = place.t, place.core
+    ff = wd.shape[0]
+    cols = sum(widths)
+    starts = (0, widths[0], widths[0] + widths[1])
+    wire = Wire(send_sem, recv_sem)
+    barrier, peers = greet(place)
+    loads = [
+        pltpu.make_async_copy(src, dst, load_sem.at[i])
+        for i, (src, dst) in enumerate(((wo_hbm, wo), (wgu_hbm, wgu), (wd_hbm, wd)))
+    ]
+    for load in loads:
+        load.start()
+    loads[0].wait()
+
+    def columns(index, start=0, size=cols):
+        return pl.ds(pl.multiple_of(index * cols + start, 128), size)
+
+    slots1 = [wire.slot() for _ in range(7)]
+    heads = att_ref[...]
+    own = None
+    for j in (4, 3, 5, 2, 6, 1, 7, 0):
+        to = lax.rem(t + j, 8)
+        part = jnp.dot(heads, wo[:, columns(to)], preferred_element_type=jnp.float32)
+        if j == 0:
+            own = part
+            break
+        s1[j - 1] = part.astype(s1.dtype)
+        if j == 4:
+            pl.semaphore_wait(barrier, peers)
+        wire.send(slots1[j - 1], s1.at[j - 1], r1.at[j - 1], {"seq": place.s, "tp": to})
+    total = own + x_ref[:, columns(t)].astype(jnp.float32)
+    for j in (1, 7, 2, 6, 3, 5, 4):
+        wire.recv(slots1[j - 1], r1.at[j - 1], {"seq": place.s, "tp": lax.rem(t + 8 - j, 8)})
+        total = total + r1[j - 1].astype(jnp.float32)
+    mine = total.astype(jnp.bfloat16)
+    mine_s[...] = mine
+
+    gs = (g0, g1, g2)
+    gathers = [Gather(wire, place, axes, buf) for axes, buf in zip(AXES, gs)]
+    for g, w, start in zip(gathers, widths, starts):
+        g.buf[core, place.at[g.c], place.at[g.b], place.at[g.a]] = mine[:, start : start + w]
+        g.open()
+    for g in gathers:
+        g.line()
+    for g in gathers:
+        g.plane_near()
+    for g in gathers:
+        g.space_near(0)
+    for g in gathers:
+        g.plane_far()
+    for db in (3, 1, 2):
+        for g in gathers:
+            g.space_near(db)
+    for db in (0, 3, 1, 2):
+        for g in gathers:
+            g.space_far(db)
+    for g in gathers:
+        g.other_core()
+
+    loads[1].wait()
+    acc[...] = jnp.zeros_like(acc)
+    squares[...] = jnp.zeros_like(squares)
+
+    def rows_of(k, c, y):
+        if k == 0:
+            v = gs[0][c, :, :, y]
+        elif k == 1:
+            v = gs[1][c, y]
+        else:
+            v = jnp.stack(
+                [jnp.stack([gs[2][c, x, y, z] for x in range(4)]) for z in range(4)]
+            )
+        return v.reshape(512, v.shape[-1])
+
+    def up_body(i, carry):
+        c, y = i // 4, i % 4
+        tt = y * 2 + c
+        for k in range(3):
+            v = rows_of(k, c, y)
+            w = wgu[columns(tt, starts[k], widths[k]), :]
+            acc[...] += jnp.dot(v, w, preferred_element_type=jnp.float32)
+            sq = None
+            for n in range(widths[k] // 128):
+                f = v[:, n * 128 : n * 128 + 128].astype(jnp.float32)
+                sq = f * f if sq is None else sq + f * f
+            squares[...] += sq
+        return carry
+
+    lax.fori_loop(0, 8, up_body, 0)
+
+    def act_body(i, carry):
+        rows = pl.ds(pl.multiple_of(i * 128, 128), 128)
+        mean = jnp.sum(squares[rows, :], axis=-1, keepdims=True) / (8 * cols)
+        r = lax.rsqrt(mean + norm_eps)
+        gate = acc[rows, :ff] * r
+        up = acc[rows, ff:] * r
+        act[rows, :] = (gate / (1.0 + jnp.exp(-gate)) * up).astype(act.dtype)
+        return carry
+
+    lax.fori_loop(0, 4, act_body, 0)
+    loads[2].wait()
+
+    ps, os_ = (p0, p1, p2), (o0, o1, o2)
+
+    def at_y(k, ref, y):
+        return ref.at[:, :, y] if k == 0 else (ref.at[y] if k == 1 else ref.at[:, y])
+
+    def down_rows(tt, z):
+        rows = act[pl.ds(pl.multiple_of(z * 128, 128), 128), :]
+        return jnp.dot(rows, wd[:, columns(tt)], preferred_element_type=jnp.float32)
+
+    slots_o = [[wire.slot() for _ in range(3)] for _ in range(4)]
+    for y in range(4):
+
+        def other_body(z, carry):
+            d = down_rows(y * 2 + 1 - core, z).astype(jnp.bfloat16).reshape(4, 32, cols)
+            ps[0][1 - core, z, :, y] = d[:, :, : widths[0]]
+            ps[1][1 - core, y, z] = d[:, :, starts[1] : starts[2]]
+            for x in range(4):
+                ps[2][1 - core, x, y, z] = d[x, :, starts[2] :]
+            return carry
+
+        lax.fori_loop(0, 4, other_body, 0)
+        for k in range(3):
+            wire.send(
+                slots_o[y][k],
+                at_y(k, ps[k].at[1 - core], y),
+                at_y(k, os_[k], y),
+                place.device(flip=True),
+            )
+    for y in range(4):
+        for k in range(3):
+            wire.recv(slots_o[y][k], at_y(k, os_[k], y), place.device(flip=True))
+
+        def own_body(z, carry):
+            d = down_rows(y * 2 + core, z).reshape(4, 32, cols)
+            d0 = d[:, :, : widths[0]] + os_[0][z, :, y].astype(jnp.float32)
+            ps[0][core, z, :, y] = d0.astype(jnp.bfloat16)
+            d1 = d[:, :, starts[1] : starts[2]] + os_[1][y, z].astype(jnp.float32)
+            ps[1][core, y, z] = d1.astype(jnp.bfloat16)
+            for x in range(4):
+                d2 = d[x, :, starts[2] :] + os_[2][x, y, z].astype(jnp.float32)
+                ps[2][core, x, y, z] = d2.astype(jnp.bfloat16)
+            return carry
+
+        lax.fori_loop(0, 4, own_body, 0)
+
+    rcs, ncs, qs = (rc0, rc1, rc2), (nc0, nc1, nc2), (q0, q1, q2)
+    rbs, nbs, tas, ras = (rb0, rb1, rb2), (nb0, nb1, nb2), (ta0, ta1, ta2), (ra0, ra1, ra2)
+
+    def piece_c(k):
+        def view(d, half):
+            at = place.shifted(AXES[k][2], d)
+            return ps[k].at[core, at, pl.ds(2 * half, 2)]
+
+        return view
+
+    def piece_b(k):
+        def view(d, half):
+            at = place.shifted(AXES[k][1], d)
+            return qs[k].at[at, pl.ds(2 * half, 2)]
+
+        return view
+
+    along_c = [
+        Scatter(wire, place, AXES[k][2], piece_c(k), rcs[k], ncs[k]) for k in range(3)
+    ]
+    along_b = [
+        Scatter(wire, place, AXES[k][1], piece_b(k), rbs[k], nbs[k]) for k in range(3)
+    ]
+    slots_a = [[wire.slot() for _ in range(3)] for _ in range(3)]
+    for s in along_c:
+        s.open()
+    for s in along_c:
+        s.pass_on(2)
+    for k, s in enumerate(along_c):
+        s.close()
+        at = place.at[AXES[k][2]]
+
+        def sum_c(b, carry):
+            v = ps[k][core, at, b].astype(jnp.float32)
+            v = v + ncs[k][0, b // 2, b % 2].astype(jnp.float32)
+            v = v + ncs[k][1, b // 2, b % 2].astype(jnp.float32)
+            qs[k][b] = v.astype(jnp.bfloat16)
+            return carry
+
+        lax.fori_loop(0, 4, sum_c, 0)
+        along_b[k].open()
+    for s in along_b:
+        s.pass_on(2)
+    for k, s in enumerate(along_b):
+        s.close()
+        at = place.at[AXES[k][1]]
+        for a in range(4):
+            v = qs[k][at, a].astype(jnp.float32)
+            v = v + nbs[k][0, a // 2, a % 2].astype(jnp.float32)
+            v = v + nbs[k][1, a // 2, a % 2].astype(jnp.float32)
+            tas[k][a] = v.astype(jnp.bfloat16)
+        for j in (2, 1, 3):
+            axis = AXES[k][0]
+            wire.send(
+                slots_a[k][j - 1],
+                tas[k].at[place.shifted(axis, j)],
+                ras[k].at[j - 1],
+                place.device(axis, j),
+            )
+    for k in range(3):
+        axis = AXES[k][0]
+        v = tas[k][place.at[axis]].astype(jnp.float32)
+        for j in (1, 3, 2):
+            wire.recv(slots_a[k][j - 1], ras[k].at[j - 1], place.device(axis, -j))
+            v = v + ras[k][j - 1].astype(jnp.float32)
+        lo = starts[k]
+        v = v + mine_s[:, lo : lo + widths[k]].astype(jnp.float32)
+        last[t, :, lo : lo + widths[k]] = v.astype(jnp.bfloat16)
+    slots_l = [wire.slot() for _ in range(7)]
+    for j in (4, 3, 5, 2, 6, 1, 7):
+        to = {"seq": place.s, "tp": lax.rem(t + j, 8)}
+        wire.send(slots_l[j - 1], last.at[t], last.at[t], to)
+    for y in range(4):
+        for c in range(2):
+            tt = y * 2 + c
+            z, x = place.at["z"], place.at["x"]
+            attended_ref[:, tt * cols : tt * cols + widths[0]] = g0[c, z, x, y]
+            attended_ref[:, tt * cols + starts[1] : tt * cols + starts[2]] = g1[c, y, z, x]
+            attended_ref[:, tt * cols + starts[2] : tt * cols + cols] = g2[c, x, y, z]
+    for j in range(1, 8):
+        tt = lax.rem(t + 8 - j, 8)
+        wire.recv(slots_l[j - 1], last.at[tt], {"seq": place.s, "tp": tt})
+    for tt in range(8):
+        layer_ref[:, tt * cols : tt * cols + cols] = last[tt]
+    wire.drain()
+
+
+def second_half(attention, x, w_output, w_gate_up, w_down):
+    rows, width = x.shape
+    cols = width // 8
+    ff = w_down.shape[0]
+    tiles = cols // 128
+    first = -(-2 * tiles // 5)
+    widths = (first * 128, first * 128, (tiles - 2 * first) * 128)
+    assert rows == 32 and min(widths) > 0
+    bf, f32 = jnp.bfloat16, jnp.float32
+    vm = pltpu.VMEM
+
+    def each(*shape):
+        return [vm(shape + (rows, w), bf) for w in widths]
+
+    count = slots_needed()
+    scratch = [
+        vm(w_output.shape, bf),
+        vm(w_gate_up.shape, bf),
+        vm(w_down.shape, bf),
+        vm((7, rows, cols), bf),
+        vm((7, rows, cols), bf),
+        *each(2, 4, 4, 4),
+        vm((512, 2 * ff), f32),
+        vm((512, 128), f32),
+        vm((512, ff), bf),
+        *each(2, 4, 4, 4),
+        *each(4, 4, 4),
+        *each(2, 2, 4),
+        *each(2, 2, 2, 4),
+        *each(4, 4),
+        *each(2, 2),
+        *each(2, 2, 2),
+        *each(4),
+        *each(3),
+        vm((rows, cols), bf),
+        vm((8, rows, cols), bf),
+        pltpu.SemaphoreType.DMA((3,)),
+        pltpu.SemaphoreType.DMA((count,)),
+        pltpu.SemaphoreType.DMA((count,)),
+    ]
+    whole = pl.BlockSpec(memory_space=pltpu.VMEM)
+    hbm = pl.BlockSpec(memory_space=pl.ANY)
+    out = jax.ShapeDtypeStruct((rows, width), bf)
+    return pl.pallas_call(
+        functools.partial(block_kernel, widths),
+        out_shape=[out, out],
+        in_specs=[whole, whole, hbm, hbm, hbm],
+        out_specs=[whole, whole],
+        scratch_shapes=scratch,
+        compiler_params=pltpu.CompilerParams(
+            collective_id=1, has_side_effects=True, vmem_limit_bytes=60 * 1024 * 1024
+        ),
+        name="second_half",
+    )(attention, x, w_output, w_gate_up, w_down)
 
 
 def local(
@@ -192,17 +758,10 @@
     attention = (acc / total[..., None]).astype(jnp.bfloat16)
     attention = jnp.swapaxes(attention.reshape(row_count, steps, group * head_dim), 0, 1)
     attention = attention.reshape(steps * row_count, group * head_dim)
-    head_part = jnp.dot(attention, w_output, preferred_element_type=jnp.float32)
-    attended = (x.astype(jnp.float32) + lax.psum(head_part, "tp")).astype(jnp.bfloat16)
-    normed_mlp = rms_norm(attended, mlp_gain).astype(jnp.bfloat16)
-    everyone = lax.all_gather(normed_mlp, "seq", axis=0, tiled=True)
-    gate = jnp.dot(everyone, w_gate, preferred_element_type=jnp.float32)
-    up = jnp.dot(everyone, w_up, preferred_element_type=jnp.float32)
-    activation = (jax.nn.silu(gate) * up).astype(jnp.bfloat16)
-    partial = jnp.dot(activation, w_down, preferred_element_type=jnp.float32)
-    mlp = lax.psum_scatter(partial, "seq", scatter_dimension=0, tiled=True)
-    mlp = lax.psum(mlp, "tp")
-    layer_out = (attended.astype(jnp.float32) + mlp).astype(jnp.bfloat16)
+    gain = mlp_gain[:, None]
+    w_gate_up = jnp.concatenate([w_gate, w_up], axis=1).astype(jnp.float32) * gain
+    w_gate_up = w_gate_up.astype(jnp.bfloat16)
+    attended, layer_out = second_half(attention, x, w_output, w_gate_up, w_down)
     shape = (steps, row_count, width)
     return attended.reshape(shape), layer_out.reshape(shape)
 

time: 396 us -> 170 us (0.43)
  waiting for transfers between devices: 287 us -> 8.91 us
  Pallas kernels: 12.8 us -> 95.3 us
  matrix products: 30.3 us -> 5.29 us
  between operations: 14 us -> 0.88 us
  local copies, waits for them, and re-layouts: 8.16 us -> 12.2 us
    psum x2 -> x0, waiting for transfers between devices: 127 us -> none  [the longest x1 65 us: local(): lax.psum(head_part, 'tp')]
    reduce_scatter x1 -> x0, waiting for transfers between devices: 89 us -> none  [local(): mlp = lax.psum_scatter(partial, 'seq', scatter_dimension=0, tiled=True)]
    pallas_call x0 -> x1, Pallas kernels: none -> 82.5 us  [second_half(): pl.pallas_call(functools.partial(block_kernel, widths), out_shape=[out, o...]
    all_gather x1 -> x0, waiting for transfers between devices: 57.9 us -> none  [local(): everyone = lax.all_gather(normed_mlp, 'seq', axis=0, tiled=True)]
    dot_general x3 -> x0, matrix products: 22.8 us -> none  [the longest x1 12.9 us: local(): partial = jnp.dot(activation, w_down, preferred_element_type=jnp.float32)]
    convert_element_type x1, other arithmetic: 0.87 us -> 6.86 us  [local(): w_gate_up = w_gate_up.astype(jnp.bfloat16)]
    all_to_all x1, waiting for transfers between devices: 4.51 us -> 0.01 us  [local(): lse = lax.all_to_all(lse.reshape(seq, row_count, head_dim), 'seq', 0, 0)]
  transfers between devices with their start and end apart: 6 -> 2, of which waited for: 6 -> 1; matrix products, arithmetic and copies ran while one was open for 1% -> 4% of each run, Pallas kernels for 0% -> 0%
where the time goes in v2:
time: 170 us; the launch traced here: 169 us
  Pallas kernels  95.3 us (56%)
  blocking collectives  22.8 us (13%)
  other arithmetic  12.4 us (7%)
  local copies, waits for them, and re-layouts  12.2 us (7%)
  starting transfers between devices  11.3 us (7%)
  waiting for transfers between devices  8.91 us (5%)
  matrix products  5.29 us (3%)
    pallas_call x1, Pallas kernels, second_half(): pl.pallas_call(functools.partial(block_kernel, widths), out_shape=[out, o...  82.5 us
    all_gather x1, blocking collectives, local(): all_q = lax.all_gather(q, 'seq', axis=0, tiled=True)  22.8 us
    pallas_call x1, Pallas kernels, paged_attention(): pl.pallas_call(functools.partial(paged_kernel, pages), grid_spec=pltpu.Pr...  12.8 us
    all_to_all x1, waiting for transfers between devices, local(): lax.all_to_all(part.reshape(seq, row_count, steps * group, head_dim), 'se...  8.91 us
    dot_general x1, local copies, waits for them, and re-layouts, local(): q = jnp.dot(normed, w_query, preferred_element_type=jnp.float32)  7.89 us
    convert_element_type x1, other arithmetic, local(): w_gate_up = w_gate_up.astype(jnp.bfloat16)  6.86 us
    all_to_all x1, starting transfers between devices, local(): lax.all_to_all(part.reshape(seq, row_count, steps * group, head_dim), 'se...  6.67 us
    all_to_all x1, starting transfers between devices, local(): lse = lax.all_to_all(lse.reshape(seq, row_count, head_dim), 'seq', 0, 0)  4.63 us
  transfers between devices with their start and end apart: 2, of which 1 were waited for; matrix products, arithmetic and copies ran while one was open for 4% of the time, Pallas kernels for 0%

profile of v2, /device:TPU:1, one launch (start us, length us, event | category | flops | bytes accessed | tf_op | source)
XLA Modules:
  0.0 169.0 jit_solution(1829931065667045350)
XLA Ops:
  0.7 0.8 compare_select_fusion.1
  1.4 0.9 select_reduce_fusion.2
  2.3 1.4 select_reduce_fusion
  3.7 1.1 fusion.5
  5.0 7.9 %copy.37 = bf16[512,5120]{1,0:T(8,128)(2,1)} copy(bf16[512,5120]{0,1:T(8,128)(2,1)} %bitcast.46) | data formatting | bytes 10485760 | tf_op jit(solution)/shard_map/dot_general | solution.py:724
  12.9 4.2 %fusion.9 = f32[32,4,128]{2,0,1:T(8,128)S(1)} fusion(bf16[4,128,5120]{2,1,0:T(8,128)(2,1)} %bitcast.44, bf16[4,8,5120]{2,1,0:T(8,128)(2,1)S(1)} %copy-done.1, f32[5120]{0:T(1024)S(1)} %copy-done.3, f32[4,8]{1,0:T(4,128)S(1)} %add_rsqrt_fusion), kind=kOutput, calls=%fused_computation.17 | convolution fusion | flops 168427520 | bytes 5656704 | tf_op jit(solution)/shard_map/dot_general | solution.py:724
  17.1 0.4 fusion.13
  17.5 0.1 fusion.25
  17.6 0.1 fusion.14
  17.8 22.8 %all_gather.3.q_ref = bf16[128,16,128]{2,1,0:T(8,128)(2,1)} all-gather(bf16[8,16,128]{2,1,0:T(8,128)(2,1)S(1)} %bitcast.52), channel_id=1, replica_groups=mesh['seq'=16,'tp'=8] {'seq'}, dimensions={0}, use_global_device_ids=true | all-gather | bytes 557056 | tf_op jit(solution)/shard_map/all_gather | solution.py:734
  40.6 0.6 compare_select_fusion.valid_ref
  41.2 12.8 %paged_attention.1 = (bf16[128,16,128]{2,1,0:T(8,128)(2,1)}, f32[128,128]{1,0:T(8,128)}) custom-call(s32[36]{0:T(128)} %get-tuple-element.11.rows_ref, s32[36]{0:T(128)} %compare_select_fusion.valid_ref, bf16[128,16,128]{2,1,0:T(8,128)(2,1)} %all_gather.3.q_ref, bf16[36,256,128]{2,1,0:T(8,128)(2,1)} %bitcast.47, bf16[36,256,128]{2,1,0:T(8,128)(2,1)} %bitcast.48), custom_call_target="tpu_custom_call" | custom-call | tf_op jit(solution)/shard_map/paged_attention/pallas_call | solution.py:91
  54.0 4.6 %all-to-all-start.1 = ((f32[16,8,128]{2,1,0:T(8,128)}), f32[16,8,128]{2,1,0:T(8,128)S(1)}, u32[]{:S(2)}, u32[]{:S(2)}) async-start(f32[16,8,128]{2,1,0:T(8,128)} %bitcast.54), calls=%async_computation.1 | async-start | bytes 131072 | tf_op jit(solution)/shard_map/all_to_all | solution.py:739
  58.7 0.4 fusion.4
  59.1 0.2 fusion.33
  59.3 6.9 %multiply_convert_fusion.wgu_hbm = bf16[5120,512]{1,0:T(8,128)(2,1)} fusion(bf16[5120,256]{1,0:T(8,128)(2,1)} %param.24, bf16[5120,256]{1,0:T(8,128)(2,1)} %param.23, f32[5120]{0:T(1024)S(1)} %copy-done.4), kind=kLoop, calls=%fused_computation | loop fusion | flops 15728640 | bytes 10506240 | tf_op jit(solution)/shard_map/convert_element_type | solution.py:763
  66.2 6.7 %all-to-all-start = ((bf16[16,8,16,128]{3,2,1,0:T(8,128)(2,1)}), bf16[16,8,16,128]{3,2,1,0:T(8,128)(2,1)S(1)}, u32[]{:S(2)}, u32[]{:S(2)}) async-start(bf16[16,8,16,128]{3,2,1,0:T(8,128)(2,1)} %bitcast.10), calls=%async_computation | async-start | bytes 1048576 | tf_op jit(solution)/shard_map/all_to_all | solution.py:738
  73.0 8.9 %all-to-all-done = bf16[16,8,16,128]{3,2,1,0:T(8,128)(2,1)S(1)} async-done(((bf16[16,8,16,128]{3,2,1,0:T(8,128)(2,1)}), bf16[16,8,16,128]{3,2,1,0:T(8,128)(2,1)S(1)}, u32[]{:S(2)}, u32[]{:S(2)}) %all-to-all-start) | async-done | bytes 524320 | tf_op jit(solution)/shard_map/all_to_all | solution.py:738
  81.9 0.3 multiply_reduce_fusion
  82.2 0.2 fusion.2
  82.4 0.6 copy.41
  83.1 82.5 %second_half.1 = (bf16[32,5120]{1,0:T(8,128)(2,1)}, bf16[32,5120]{1,0:T(8,128)(2,1)}) custom-call(bf16[32,512]{1,0:T(8,128)(2,1)} %bitcast.51, bf16[32,5120]{1,0:T(8,128)(2,1)} %bitcast.45, bf16[512,5120]{1,0:T(8,128)(2,1)} %wo_hbm.1, bf16[5120,512]{1,0:T(8,128)(2,1)} %multiply_convert_fusion.wgu_hbm, bf16[256,5120]{1,0:T(8,128)(2,1)} %wd_hbm.1), custom_call_target="tpu_custom_call" | custom-call | tf_op jit(solution)/shard_map/second_half/pallas_call | solution.py:672
  165.6 1.7 %copy.44 = bf16[4,8,5120]{2,1,0:T(8,128)(2,1)} copy(bf16[4,8,5120]{2,1,0:T(8,128)(2,1)} %bitcast.50) | data formatting | bytes 655360
  167.3 1.7 %copy.45 = bf16[4,8,5120]{2,1,0:T(8,128)(2,1)} copy(bf16[4,8,5120]{2,1,0:T(8,128)(2,1)} %bitcast.49) | data formatting | bytes 655360
  (33 shorter events, 0.5 us)
Async XLA Ops:
  0.6 16.4 %copy-start = (bf16[5120,128]{1,0:T(8,128)(2,1)S(1)}, bf16[5120,128]{1,0:T(8,128)(2,1)}, u32[]{:S(2)}) copy-start(bf16[5120,128]{1,0:T(8,128)(2,1)} %param.19) | copy-start | bytes 3932164
  5.0 7.9 %copy-start.1 = (bf16[4,8,5120]{2,1,0:T(8,128)(2,1)S(1)}, bf16[4,8,5120]{2,1,0:T(8,128)(2,1)}, u32[]{:S(2)}) copy-start(bf16[4,8,5120]{2,1,0:T(8,128)(2,1)} %param.16) | copy-start | bytes 983044
  5.0 7.9 %copy-start.3 = (f32[5120]{0:T(1024)S(1)}, f32[5120]{0:T(1024)}, u32[]{:S(2)}) copy-start(f32[5120]{0:T(1024)} %param.17) | copy-start | bytes 61444
  12.9 27.7 %copy-start.5 = (s32[36]{0:T(128)S(1)}, s32[36]{0:T(128)}, u32[]{:S(2)}) copy-start(s32[36]{0:T(128)} %param.29) | copy-start | bytes 436
  12.9 27.8 %copy-start.6 = (s32[36]{0:T(128)S(1)}, s32[36]{0:T(128)}, u32[]{:S(2)}) copy-start(s32[36]{0:T(128)} %param.30) | copy-start | bytes 436
  17.1 41.6 %copy-start.2 = (bf16[5120,128]{1,0:T(8,128)(2,1)S(1)}, bf16[5120,128]{1,0:T(8,128)(2,1)}, u32[]{:S(2)}) copy-start(bf16[5120,128]{1,0:T(8,128)(2,1)} %param.20) | copy-start | bytes 3932164
  17.1 42.2 %copy-start.4 = (f32[5120]{0:T(1024)S(1)}, f32[5120]{0:T(1024)}, u32[]{:S(2)}) copy-start(f32[5120]{0:T(1024)} %param.22) | copy-start | bytes 61444
  54.0 12.2 %all-to-all-start.1 = ((f32[16,8,128]{2,1,0:T(8,128)}), f32[16,8,128]{2,1,0:T(8,128)S(1)}, u32[]{:S(2)}, u32[]{:S(2)}) async-start(f32[16,8,128]{2,1,0:T(8,128)} %bitcast.54), calls=%async_computation.1 | async-start | bytes 131072 | tf_op jit(solution)/shard_map/all_to_all | solution.py:739
  66.2 15.7 %all-to-all-start = ((bf16[16,8,16,128]{3,2,1,0:T(8,128)(2,1)}), bf16[16,8,16,128]{3,2,1,0:T(8,128)(2,1)S(1)}, u32[]{:S(2)}, u32[]{:S(2)}) async-start(bf16[16,8,16,128]{3,2,1,0:T(8,128)(2,1)} %bitcast.10), calls=%async_computation | async-start | bytes 1048576 | tf_op jit(solution)/shard_map/all_to_all | solution.py:738

commit v3 on v2

--- a/solution.py
+++ b/solution.py
@@ -13,30 +13,12 @@
 masked_low = -1e30
 
 
-def rms_norm(values, gain):
-    floats = values.astype(jnp.float32)
-    square_mean = jnp.mean(floats * floats, axis=-1, keepdims=True)
-    return floats * lax.rsqrt(square_mean + norm_eps) * gain
-
-
-def rotary_tables(token_position, head_dim):
-    half_dim = head_dim // 2
-    exponent = jnp.arange(half_dim, dtype=jnp.float32) * (2.0 / head_dim)
-    inverse_freq = rope_theta ** (-exponent)
-    angles = token_position.astype(jnp.float32)[:, None] * inverse_freq[None, :]
-    return jnp.cos(angles), jnp.sin(angles)
-
-
-def rotate(values, cosine, sine):
-    half = values.shape[-1] // 2
-    a = values[..., :half]
-    b = values[..., half:]
-    return jnp.concatenate([a * cosine - b * sine, b * cosine + a * sine], axis=-1)
-
-
-def paged_kernel(pages, rows_ref, valid_ref, q_ref, k_ref, v_ref, o_ref, lse_ref, m_s, l_s, acc_s):
+def paged_kernel(
+    pages, request_ref, number_ref, slot_ref, length_ref, q_ref, k_ref, v_ref, o_ref, lse_ref, m_s, l_s, acc_s
+):
     step = pl.program_id(0)
     scale = k_ref.shape[-1] ** (-0.5)
+    length = k_ref.shape[1]
 
     @pl.when(step == 0)
     def _():
@@ -47,9 +29,13 @@
     stats = []
     for i in range(pages):
         page = step * pages + i
-        row = rows_ref[page]
-        valid = valid_ref[page]
-        q = q_ref[row]
+        request = request_ref[page]
+        live_page = request >= 0
+        request = jnp.maximum(request, 0)
+        row = slot_ref[request]
+        valid = jnp.clip(length_ref[request] - number_ref[page] * length, 0, length)
+        valid = jnp.where(live_page, valid, 0)
+        q = q_ref[(row % 8) // 4, row // 8, row % 4]
         s = (
             lax.dot_general(
                 q, k_ref[i], (((1,), (1,)), ((), ())), preferred_element_type=jnp.float32
@@ -78,25 +64,38 @@
         safe = jnp.where(l > 0.0, l, 1.0)
         o_ref[...] = (acc_s[...] / safe).astype(o_ref.dtype)
         lse = jnp.where(l > 0.0, m_s[...] + jnp.log(safe), masked_low)
-        eye = lax.broadcasted_iota(jnp.int32, lse.shape, 1) == lax.broadcasted_iota(
-            jnp.int32, lse.shape, 2
-        )
-        lse_ref[...] = jnp.sum(jnp.where(eye, lse, 0.0), axis=1)
-
-
-def paged_attention(rows, valid, queries, keys, values):
-    total, group, dim = queries.shape
-    count, length, _ = keys.shape
+        lse_ref[...] = compact(lse)
+
+
+def compact(values):
+    eye = lax.broadcasted_iota(jnp.int32, values.shape, 1) == lax.broadcasted_iota(
+        jnp.int32, values.shape, 2
+    )
+    return jnp.sum(jnp.where(eye, values, 0.0), axis=1)
+
+
+def expand(values, count):
+    shape = (values.shape[0], count, values.shape[1])
+    eye = lax.broadcasted_iota(jnp.int32, shape, 1) == lax.broadcasted_iota(jnp.int32, shape, 2)
+    wide = jnp.broadcast_to(values[:, None, :], shape)
+    return jnp.sum(jnp.where(eye, wide, 0.0), axis=-1, keepdims=True)
+
+
+def paged_attention(request, number, slot, lengths, queries, keys, values):
+    group, dim = queries.shape[-2:]
+    total = slot.shape[0]
+    count, _, length, _ = keys.shape
     pages = next(n for n in (6, 4, 3, 2, 1) if count % n == 0)
+    paged = pl.BlockSpec((pages, None, length, dim), lambda i, *_: (i, 0, 0, 0))
     return pl.pallas_call(
         functools.partial(paged_kernel, pages),
         grid_spec=pltpu.PrefetchScalarGridSpec(
-            num_scalar_prefetch=2,
+            num_scalar_prefetch=4,
             grid=(count // pages,),
             in_specs=[
-                pl.BlockSpec((total, group, dim), lambda i, *_: (0, 0, 0)),
-                pl.BlockSpec((pages, length, dim), lambda i, *_: (i, 0, 0)),
-                pl.BlockSpec((pages, length, dim), lambda i, *_: (i, 0, 0)),
+                pl.BlockSpec(queries.shape, lambda i, *_: (0, 0, 0, 0, 0)),
+                paged,
+                paged,
             ],
             out_specs=[
                 pl.BlockSpec((total, group, dim), lambda i, *_: (0, 0, 0)),
@@ -113,7 +112,7 @@
             jax.ShapeDtypeStruct((total, dim), jnp.float32),
         ],
         name="paged_attention",
-    )(rows, valid, queries, keys, values)
+    )(request, number, slot, lengths, queries, keys, values)
 
 
 AXES = (("y", "x", "z"), ("x", "z", "y"), ("z", "y", "x"))
@@ -181,10 +180,24 @@
 def greet(place):
     barrier = pltpu.get_barrier_semaphore()
     peers = [{"seq": place.s, "tp": lax.rem(place.t + j, 8)} for j in range(1, 8)]
-    peers += [place.device(axis, by) for axis in ("x", "z") for by in (1, 2, 3)]
+    peers += [{"seq": seq_peer(place, j)[0], "tp": place.t} for j in SEQ_ORDER]
     for peer in peers:
         pl.semaphore_signal(barrier, inc=1, device_id=peer, device_id_type=MESH)
     return barrier, len(peers)
+
+
+SEQ_ORDER = tuple(
+    sorted(
+        ((dz, dx) for dz in range(4) for dx in range(4) if (dz, dx) != (0, 0)),
+        key=lambda d: -(min(d[0], 4 - d[0]) + min(d[1], 4 - d[1])),
+    )
+)
+
+
+def seq_peer(place, by):
+    on = place.shifted("z", by[0]) * 4 + place.shifted("x", by[1])
+    back = place.shifted("z", -by[0]) * 4 + place.shifted("x", -by[1])
+    return on, back
 
 
 class Gather:
@@ -327,23 +340,20 @@
 
 
 def slots_needed():
-    class Count:
-        def __init__(self):
-            self.n = 0
-
-        def slot(self):
-            self.n += 1
-            return self.n - 1
-
-    return 7 + 3 * (3 + 4 + 16 + 16) + 12 + 3 * (6 + 6 + 3) + 7
+    return 30 + 7 + 3 * (3 + 4 + 16 + 16) + 12 + 3 * (6 + 6 + 3) + 7
 
 
 def block_kernel(
     widths,
-    att_ref,
+    part_ref,
+    lse_ref,
+    fresh_ref,
+    fresh_lse_ref,
     x_ref,
+    gain_ref,
     wo_hbm,
-    wgu_hbm,
+    wg_hbm,
+    wu_hbm,
     wd_hbm,
     attended_ref,
     layer_ref,
@@ -387,6 +397,9 @@
     ra2,
     mine_s,
     last,
+    parts,
+    lses,
+    att32,
     load_sem,
     send_sem,
     recv_sem,
@@ -398,19 +411,73 @@
     starts = (0, widths[0], widths[0] + widths[1])
     wire = Wire(send_sem, recv_sem)
     barrier, peers = greet(place)
+    weights = (
+        (wg_hbm, wgu.at[:, pl.ds(0, ff)]),
+        (wu_hbm, wgu.at[:, pl.ds(ff, ff)]),
+        (wo_hbm, wo),
+        (wd_hbm, wd),
+    )
     loads = [
-        pltpu.make_async_copy(src, dst, load_sem.at[i])
-        for i, (src, dst) in enumerate(((wo_hbm, wo), (wgu_hbm, wgu), (wd_hbm, wd)))
+        pltpu.make_async_copy(src, dst, load_sem.at[i]) for i, (src, dst) in enumerate(weights)
     ]
     for load in loads:
         load.start()
-    loads[0].wait()
 
     def columns(index, start=0, size=cols):
         return pl.ds(pl.multiple_of(index * cols + start, 128), size)
 
+    slots_e = [[wire.slot() for _ in range(2)] for _ in range(15)]
+    pl.semaphore_wait(barrier, peers)
+    for n, j in enumerate(SEQ_ORDER):
+        to, _ = seq_peer(place, j)
+        device = {"seq": to, "tp": t}
+        wire.send(slots_e[n][0], part_ref.at[to], parts.at[n], device)
+        wire.send(slots_e[n][1], lse_ref.at[to], lses.at[n], device)
+
+    loads[0].wait()
+    loads[1].wait()
+
+    def gain_body(n, carry):
+        rows = pl.ds(pl.multiple_of(n * 128, 128), 128)
+        row = jnp.broadcast_to(gain_ref[pl.ds(n, 1), :], (128, 128))
+        eye = lax.broadcasted_iota(jnp.int32, row.shape, 0) == lax.broadcasted_iota(
+            jnp.int32, row.shape, 1
+        )
+        column = jnp.sum(jnp.where(eye, row, 0.0), axis=1, keepdims=True)
+        wgu[rows, :] = (wgu[rows, :].astype(jnp.float32) * column).astype(wgu.dtype)
+        return carry
+
+    lax.fori_loop(0, wgu.shape[0] // 128, gain_body, 0)
+
+    for n, j in enumerate(SEQ_ORDER):
+        _, back = seq_peer(place, j)
+        device = {"seq": back, "tp": t}
+        wire.recv(slots_e[n][0], parts.at[n], device)
+        wire.recv(slots_e[n][1], lses.at[n], device)
+    count = part_ref.shape[2]
+    sums = [lses[n] for n in range(15)] + [lse_ref[place.s], fresh_lse_ref[...]]
+    top = functools.reduce(jnp.maximum, sums)
+    sums = [jnp.exp(v - top) for v in sums]
+    whole = functools.reduce(jnp.add, sums)
+    attention = fresh_ref[...] * expand(sums[16] / whole, count)
+    for n in range(15):
+        attention += parts[n].astype(jnp.float32) * expand(sums[n] / whole, count)
+    attention += part_ref[place.s].astype(jnp.float32) * expand(sums[15] / whole, count)
+    att32[...] = attention
+    per_step = count // STEPS
+    heads = jnp.concatenate(
+        [
+            jnp.concatenate(
+                [att32[:, i * per_step + g, :].astype(jnp.bfloat16) for g in range(per_step)],
+                axis=1,
+            )
+            for i in range(STEPS)
+        ],
+        axis=0,
+    )
+
     slots1 = [wire.slot() for _ in range(7)]
-    heads = att_ref[...]
+    loads[2].wait()
     own = None
     for j in (4, 3, 5, 2, 6, 1, 7, 0):
         to = lax.rem(t + j, 8)
@@ -419,8 +486,6 @@
             own = part
             break
         s1[j - 1] = part.astype(s1.dtype)
-        if j == 4:
-            pl.semaphore_wait(barrier, peers)
         wire.send(slots1[j - 1], s1.at[j - 1], r1.at[j - 1], {"seq": place.s, "tp": to})
     total = own + x_ref[:, columns(t)].astype(jnp.float32)
     for j in (1, 7, 2, 6, 3, 5, 4):
@@ -451,7 +516,6 @@
     for g in gathers:
         g.other_core()
 
-    loads[1].wait()
     acc[...] = jnp.zeros_like(acc)
     squares[...] = jnp.zeros_like(squares)
 
@@ -492,7 +556,7 @@
         return carry
 
     lax.fori_loop(0, 4, act_body, 0)
-    loads[2].wait()
+    loads[3].wait()
 
     ps, os_ = (p0, p1, p2), (o0, o1, o2)
 
@@ -626,7 +690,7 @@
     wire.drain()
 
 
-def second_half(attention, x, w_output, w_gate_up, w_down):
+def second_half(part, lse, fresh, fresh_lse, x, gain, w_output, w_gate, w_up, w_down):
     rows, width = x.shape
     cols = width // 8
     ff = w_down.shape[0]
@@ -643,7 +707,7 @@
     count = slots_needed()
     scratch = [
         vm(w_output.shape, bf),
-        vm(w_gate_up.shape, bf),
+        vm((width, 2 * ff), bf),
         vm(w_down.shape, bf),
         vm((7, rows, cols), bf),
         vm((7, rows, cols), bf),
@@ -662,7 +726,10 @@
         *each(3),
         vm((rows, cols), bf),
         vm((8, rows, cols), bf),
-        pltpu.SemaphoreType.DMA((3,)),
+        vm((15,) + part.shape[1:], bf),
+        vm((15,) + lse.shape[1:], f32),
+        vm(part.shape[1:], f32),
+        pltpu.SemaphoreType.DMA((4,)),
         pltpu.SemaphoreType.DMA((count,)),
         pltpu.SemaphoreType.DMA((count,)),
     ]
@@ -672,14 +739,214 @@
     return pl.pallas_call(
         functools.partial(block_kernel, widths),
         out_shape=[out, out],
-        in_specs=[whole, whole, hbm, hbm, hbm],
+        in_specs=[whole] * 6 + [hbm] * 4,
         out_specs=[whole, whole],
         scratch_shapes=scratch,
         compiler_params=pltpu.CompilerParams(
             collective_id=1, has_side_effects=True, vmem_limit_bytes=60 * 1024 * 1024
         ),
         name="second_half",
-    )(attention, x, w_output, w_gate_up, w_down)
+    )(part, lse, fresh, fresh_lse, x, gain, w_output, w_gate, w_up, w_down)
+
+
+class QueryGather:
+    def __init__(self, wire, place, axes, buf):
+        self.wire, self.place, self.buf = wire, place, buf
+        self.a, self.b = axes
+        self.slots_a = [wire.slot() for _ in range(3)]
+        self.slots_b = [wire.slot() for _ in range(4)]
+
+    def cut(self, b, a):
+        return self.buf.at[b, a] if self.b == "z" else self.buf.at[a, b]
+
+    def block(self, da):
+        return self.cut(self.place.at[self.b], self.place.shifted(self.a, da))
+
+    def half(self, db, which):
+        return self.cut(self.place.shifted(self.b, db), pl.ds(2 * which, 2))
+
+    def group(self, db):
+        return self.cut(self.place.shifted(self.b, db), pl.ds(0, 4))
+
+    def open(self):
+        mine = self.block(0)
+        for j in (2, 1, 3):
+            self.wire.send(self.slots_a[j - 1], mine, mine, self.place.device(self.a, j))
+
+    def line(self):
+        for j in (1, 3, 2):
+            self.wire.recv(self.slots_a[j - 1], self.block(-j), self.place.device(self.a, -j))
+        mine = self.group(0)
+        self.wire.send(self.slots_b[0], mine, mine, self.place.device(self.b, 1))
+        self.wire.send(self.slots_b[1], mine, mine, self.place.device(self.b, -1))
+
+    def near(self):
+        place, wire = self.place, self.wire
+        wire.recv(self.slots_b[0], self.group(-1), place.device(self.b, -1))
+        part = self.half(-1, 0)
+        wire.send(self.slots_b[2], part, part, place.device(self.b, 1))
+        wire.recv(self.slots_b[1], self.group(1), place.device(self.b, 1))
+        part = self.half(1, 1)
+        wire.send(self.slots_b[3], part, part, place.device(self.b, -1))
+
+    def far(self):
+        place, wire = self.place, self.wire
+        wire.recv(self.slots_b[2], self.half(2, 0), place.device(self.b, -1))
+        wire.recv(self.slots_b[3], self.half(2, 1), place.device(self.b, 1))
+
+
+def project_kernel(
+    x_ref,
+    gain_ref,
+    freq_ref,
+    slot_ref,
+    length_ref,
+    wq_hbm,
+    wk_hbm,
+    wv_hbm,
+    q_all,
+    fresh_ref,
+    fresh_lse_ref,
+    wq,
+    wk,
+    wv,
+    q32,
+    load_sem,
+    send_sem,
+    recv_sem,
+):
+    place = Place()
+    wire = Wire(send_sem, recv_sem)
+    rows, width = x_ref.shape
+    dim = wk.shape[1]
+    heads = wq.shape[1] // dim
+    steps = STEPS
+    own = rows // steps
+    barrier = pltpu.get_barrier_semaphore()
+    for axis in ("x", "z"):
+        for by in (1, 2, 3):
+            pl.semaphore_signal(
+                barrier, inc=1, device_id=place.device(axis, by), device_id_type=MESH
+            )
+    chunks = load_sem.shape[0]
+    depth = width // chunks
+    loads = []
+    for i in range(chunks):
+        part = pl.ds(i * depth, depth)
+        loads.append(
+            [
+                pltpu.make_async_copy(src.at[part], dst.at[part], load_sem.at[i, n])
+                for n, (src, dst) in enumerate(((wq_hbm, wq), (wk_hbm, wk), (wv_hbm, wv)))
+            ]
+        )
+        for load in loads[-1]:
+            load.start()
+    x = x_ref[...].astype(jnp.float32)
+    mean = jnp.mean(x * x, axis=-1, keepdims=True)
+    normed = (x * lax.rsqrt(mean + norm_eps) * gain_ref[...]).astype(jnp.bfloat16)
+
+    shape = (own, slot_ref.shape[1])
+    mine = place.s * own + lax.broadcasted_iota(jnp.int32, shape, 0)
+    length = jnp.where(slot_ref[...] == mine, length_ref[...].astype(jnp.float32), 0.0)
+    length = jnp.sum(length, axis=-1, keepdims=True)
+    position = jnp.concatenate([length + float(i) for i in range(steps)], axis=0)
+    angle = position * freq_ref[...]
+    cosine = jnp.cos(angle)
+    sine = jnp.sin(angle)
+    low = lax.broadcasted_iota(jnp.int32, angle.shape, 1) < dim // 2
+    sine = jnp.where(low, -sine, sine)
+
+    def rotate(v):
+        return v * cosine + pltpu.roll(v, dim // 2, 1) * sine
+
+    q = k = v = 0.0
+    for i in range(chunks):
+        for load in loads[i]:
+            load.wait()
+        lhs = normed[:, i * depth : (i + 1) * depth]
+        part = pl.ds(i * depth, depth)
+        q = q + jnp.dot(lhs, wq[part, :], preferred_element_type=jnp.float32)
+        k = k + jnp.dot(lhs, wk[part, :], preferred_element_type=jnp.float32)
+        v = v + jnp.dot(lhs, wv[part, :], preferred_element_type=jnp.float32)
+    for g in range(heads):
+        turned = rotate(q[:, g * dim : (g + 1) * dim])
+        for i in range(steps):
+            q32[:, i * heads + g, :] = turned[i * own : (i + 1) * own]
+    queries = q32[...].astype(jnp.bfloat16)
+    s_at = (place.at["z"], place.at["x"])
+    half = own // 2
+    for n in range(2):
+        q_all[n, s_at[0], s_at[1]] = queries[n * half : (n + 1) * half]
+    gathers = [
+        QueryGather(wire, place, axes, q_all.at[n])
+        for n, axes in enumerate((("x", "z"), ("z", "x")))
+    ]
+    pl.semaphore_wait(barrier, 6)
+    for g in gathers:
+        g.open()
+
+    new_k = rotate(k).astype(jnp.bfloat16)
+    new_v = v.astype(jnp.bfloat16)
+    count = steps * heads
+    flat = queries.reshape(own * count, dim)
+    s = lax.dot_general(
+        flat, new_k, (((1,), (1,)), ((), ())), preferred_element_type=jnp.float32
+    ) * (dim**-0.5)
+    r = lax.broadcasted_iota(jnp.int32, s.shape, 0)
+    c = lax.broadcasted_iota(jnp.int32, s.shape, 1)
+    allowed = (r // count == c % own) & (c // own <= (r % count) // heads)
+    s = jnp.where(allowed, s, masked_low)
+    top = jnp.max(s, axis=-1, keepdims=True)
+    w = jnp.where(allowed, jnp.exp(s - top), 0.0)
+    total = jnp.sum(w, axis=-1, keepdims=True)
+    acc = jnp.dot(w.astype(jnp.bfloat16), new_v, preferred_element_type=jnp.float32)
+    fresh_ref[...] = (acc / total).reshape(own, count, dim)
+    lse = jnp.broadcast_to(top + jnp.log(total), (own * count, dim))
+    fresh_lse_ref[...] = compact(lse.reshape(own, count, dim))
+
+    for g in gathers:
+        g.line()
+    for g in gathers:
+        g.near()
+    for g in gathers:
+        g.far()
+    wire.drain()
+
+
+def first_half(x, gain, slot, lengths, w_query, w_key, w_value):
+    rows, width = x.shape
+    dim = w_key.shape[1]
+    count = STEPS * w_query.shape[1] // dim
+    own = rows // STEPS
+    bf, f32, vm = jnp.bfloat16, jnp.float32, pltpu.VMEM
+    exponent = jnp.arange(dim // 2, dtype=f32) * (2.0 / dim)
+    freq = rope_theta ** (-exponent)
+    freq = jnp.concatenate([freq, freq])[None, :]
+    whole = pl.BlockSpec(memory_space=pltpu.VMEM)
+    hbm = pl.BlockSpec(memory_space=pl.ANY)
+    return pl.pallas_call(
+        project_kernel,
+        out_shape=[
+            jax.ShapeDtypeStruct((2, 4, 4, own // 2, count, dim), bf),
+            jax.ShapeDtypeStruct((own, count, dim), f32),
+            jax.ShapeDtypeStruct((own, dim), f32),
+        ],
+        in_specs=[whole] * 5 + [hbm] * 3,
+        out_specs=[whole] * 3,
+        scratch_shapes=[
+            vm(w_query.shape, bf),
+            vm(w_key.shape, bf),
+            vm(w_value.shape, bf),
+            vm((own, count, dim), f32),
+            pltpu.SemaphoreType.DMA((8, 3)),
+            pltpu.SemaphoreType.DMA((14,)),
+            pltpu.SemaphoreType.DMA((14,)),
+        ],
+        compiler_params=pltpu.CompilerParams(
+            collective_id=2, has_side_effects=True, vmem_limit_bytes=40 * 1024 * 1024
+        ),
+        name="first_half",
+    )(x, gain[None, :], freq, slot[None, :], lengths[None, :], w_query, w_key, w_value)
 
 
 def local(
@@ -701,67 +968,34 @@
     request_slot,
 ):
     steps, row_count, width = token_inputs.shape
+    x = token_inputs.reshape(steps * row_count, width)
+    queries, fresh, fresh_lse = first_half(
+        x, attn_gain, request_slot, cache_lengths, w_query, key_projection, value_projection
+    )
+    count, dim = queries.shape[-2:]
     seq = lax.axis_size("seq")
-    total_rows = row_count * seq
-    page_count, kv_local, page_size, head_dim = key_cache.shape
-    group = w_query.shape[1] // head_dim
-    scale = head_dim ** (-0.5)
-    first_row = lax.axis_index("seq") * row_count
-    own_rows = first_row + jnp.arange(row_count, dtype=jnp.int32)
-    own_match = request_slot[None, :] == own_rows[:, None]
-    row_lengths = jnp.sum(jnp.where(own_match, cache_lengths[None, :], 0), axis=1)
-    page_live = page_request >= 0
-    page_req = jnp.where(page_live, page_request, 0)
-    req_match = page_req[:, None] == jnp.arange(total_rows, dtype=jnp.int32)[None, :]
-    page_row = jnp.sum(jnp.where(req_match, request_slot[None, :], 0), axis=1)
-    page_len = jnp.sum(jnp.where(req_match, cache_lengths[None, :], 0), axis=1)
-    valid = jnp.where(page_live, jnp.clip(page_len - page_number * page_size, 0, page_size), 0)
-
-    x = token_inputs.reshape(steps * row_count, width)
-    normed = rms_norm(x, attn_gain).astype(jnp.bfloat16)
-    position = (jnp.arange(steps, dtype=jnp.int32)[:, None] + row_lengths[None, :]).reshape(-1)
-    cosine, sine = rotary_tables(position, head_dim)
-    q = jnp.dot(normed, w_query, preferred_element_type=jnp.float32)
-    q = rotate(q.reshape(-1, group, head_dim), cosine[:, None], sine[:, None])
-    q = q.astype(jnp.bfloat16).reshape(steps, row_count, group, head_dim)
-    fresh_k = rotate(
-        jnp.dot(normed, key_projection, preferred_element_type=jnp.float32), cosine, sine
+    queries = queries.reshape(2, seq, row_count // 2, count, dim)
+    part, lse = paged_attention(
+        page_request,
+        page_number,
+        request_slot,
+        cache_lengths,
+        queries,
+        key_cache,
+        paged_value_cache,
     )
-    fresh_k = fresh_k.astype(jnp.bfloat16).reshape(steps, row_count, head_dim)
-    fresh_v = jnp.dot(normed, value_projection, preferred_element_type=jnp.float32)
-    fresh_v = fresh_v.astype(jnp.bfloat16).reshape(steps, row_count, head_dim)
-    q = jnp.swapaxes(q, 0, 1).reshape(row_count, steps * group, head_dim)
-    all_q = lax.all_gather(q, "seq", axis=0, tiled=True)
-    part, lse = paged_attention(
-        page_row, valid, all_q, key_cache[:, 0], paged_value_cache[:, 0]
+    attended, layer_out = second_half(
+        part.reshape(seq, row_count, count, dim),
+        lse.reshape(seq, row_count, dim),
+        fresh,
+        fresh_lse,
+        x,
+        mlp_gain.reshape(-1, 128),
+        w_output,
+        w_gate,
+        w_up,
+        w_down,
     )
-    part = lax.all_to_all(part.reshape(seq, row_count, steps * group, head_dim), "seq", 0, 0)
-    lse = lax.all_to_all(lse.reshape(seq, row_count, head_dim), "seq", 0, 0)
-    lse = lse[:, :, : steps * group]
-    s = jnp.einsum("rqd,jrd->rqj", q, fresh_k, preferred_element_type=jnp.float32) * scale
-    allowed = (
-        jnp.arange(steps)[None, :] <= (jnp.arange(steps * group) // group)[:, None]
-    )
-    s = jnp.where(allowed[None], s, masked_low)
-    recent_max = jnp.max(s, axis=-1)
-    w = jnp.where(allowed[None], jnp.exp(s - recent_max[..., None]), 0.0)
-    recent_sum = jnp.sum(w, axis=-1)
-    recent_acc = jnp.einsum(
-        "rqj,jrd->rqd", w.astype(jnp.bfloat16), fresh_v, preferred_element_type=jnp.float32
-    )
-    top = jnp.maximum(jnp.max(lse, axis=0), recent_max)
-    factor = jnp.exp(lse - top[None])
-    fresh_factor = jnp.exp(recent_max - top)
-    total = jnp.sum(factor, axis=0) + recent_sum * fresh_factor
-    acc = jnp.sum(part.astype(jnp.float32) * factor[..., None], axis=0)
-    acc = acc + recent_acc * fresh_factor[..., None]
-    attention = (acc / total[..., None]).astype(jnp.bfloat16)
-    attention = jnp.swapaxes(attention.reshape(row_count, steps, group * head_dim), 0, 1)
-    attention = attention.reshape(steps * row_count, group * head_dim)
-    gain = mlp_gain[:, None]
-    w_gate_up = jnp.concatenate([w_gate, w_up], axis=1).astype(jnp.float32) * gain
-    w_gate_up = w_gate_up.astype(jnp.bfloat16)
-    attended, layer_out = second_half(attention, x, w_output, w_gate_up, w_down)
     shape = (steps, row_count, width)
     return attended.reshape(shape), layer_out.reshape(shape)
 

time: 170 us -> 137 us (0.81)
  Pallas kernels: 95.3 us -> 123 us
  blocking collectives: 22.8 us -> 0 us
  other arithmetic: 12.4 us -> 0.09 us
  starting transfers between devices: 11.3 us -> 0 us
  waiting for transfers between devices: 8.91 us -> 0 us
  matrix products: 5.29 us -> 0 us
    all_gather x1 -> x0, blocking collectives: 22.8 us -> none  [local(): all_q = lax.all_gather(q, 'seq', axis=0, tiled=True)]
    pallas_call x0 -> x1, Pallas kernels: none -> 21.1 us  [first_half(): pl.pallas_call(project_kernel, out_shape=[jax.ShapeDtypeStruct((2, 4, 4,...]
    all_to_all x2 -> x0, starting transfers between devices: 11.3 us -> none  [the longest x1 6.67 us: local(): lax.all_to_all(part.reshape(seq, row_count, steps * group, head_dim), 'se...]
    unnamed x16 -> x22, local copies, waits for them, and re-layouts: 3.47 us -> 13.6 us
    all_to_all x2 -> x0, waiting for transfers between devices: 8.91 us -> none  [the longest x1 8.91 us: local(): lax.all_to_all(part.reshape(seq, row_count, steps * group, head_dim), 'se...]
    dot_general x1 -> x0, local copies, waits for them, and re-layouts: 7.89 us -> none  [local(): q = jnp.dot(normed, w_query, preferred_element_type=jnp.float32)]
    convert_element_type x2 -> x0, other arithmetic: 6.87 us -> none  [the longest x1 6.86 us: local(): w_gate_up = w_gate_up.astype(jnp.bfloat16)]
    pallas_call x1, Pallas kernels: 82.5 us -> 88.7 us  [second_half(): pl.pallas_call(functools.partial(block_kernel, widths), out_shape=[out, o...]
  transfers between devices with their start and end apart: 2 -> 0, of which waited for: 1 -> 0; matrix products, arithmetic and copies ran while one was open for 4% -> 0% of each run, Pallas kernels for 0% -> 0%
where the time goes in v3:
time: 137 us
  Pallas kernels  123 us (90%)
  local copies, waits for them, and re-layouts  13.6 us (10%)
    pallas_call x1, Pallas kernels, second_half(): pl.pallas_call(functools.partial(block_kernel, widths), out_shape=[out, o...  88.7 us
    pallas_call x1, Pallas kernels, first_half(): pl.pallas_call(project_kernel, out_shape=[jax.ShapeDtypeStruct((2, 4, 4,...  21.1 us
    unnamed x22, local copies, waits for them, and re-layouts  13.6 us
    pallas_call x1, Pallas kernels, paged_attention(): pl.pallas_call(functools.partial(paged_kernel, pages), grid_spec=pltpu.Pr...  12.8 us

profile of v3, /device:TPU:1, one launch (start us, length us, event | category | flops | bytes accessed | tf_op | source)
XLA Modules:
  0.0 136.9 jit_solution(5831557379108101091)
XLA Ops:
  0.6 0.1 maximum_bitcast_fusion.freq_ref
  0.7 0.0 copy-start
  0.7 2.5 %copy-done = bf16[5120,512]{1,0:T(8,128)(2,1)S(1)} copy-done((bf16[5120,512]{1,0:T(8,128)(2,1)S(1)}, bf16[5120,512]{1,0:T(8,128)(2,1)}, u32[]{:S(2)}) %copy-start) | copy-done | bytes 5242904
  3.2 0.0 copy-start.1
  3.2 1.3 copy-done.1
  4.5 0.0 copy-start.2
  4.5 1.3 copy-done.2
  5.8 0.0 copy-start.3
  5.8 1.0 copy-done.3
  6.8 0.0 copy-start.6
  6.8 0.7 copy-done.6
  7.5 0.0 copy-start.8
  7.5 0.7 copy-done.8
  8.2 0.0 copy-start.9
  8.2 0.7 copy-done.9
  8.9 21.1 %first_half.1 = (bf16[2,4,4,4,16,128]{5,4,3,2,1,0:T(8,128)(2,1)S(1)}, f32[8,16,128]{2,1,0:T(8,128)S(1)}, f32[8,128]{1,0:T(8,128)S(1)}) custom-call(bf16[32,5120]{1,0:T(8,128)(2,1)S(1)} %bitcast.13, f32[1,5120]{1,0:T(1,128)S(1)} %bitcast.15, f32[1,128]{1,0:T(1,128)S(1)} %maximum_bitcast_fusion.freq_ref, s32[1,128]{1,0:T(1,128)S(1)} %bitcast.16, ...), custom_call_target="tpu_custom_call" | custom-call | tf_op jit(solution)/shard_map/first_half/pallas_call | solution.py:927
  30.0 0.0 copy-start.4
  30.0 0.8 copy-done.4
  30.8 0.6 copy-done.5
  31.4 0.6 copy-done.7
  32.0 12.8 %paged_attention.1 = (bf16[128,16,128]{2,1,0:T(8,128)(2,1)}, f32[128,128]{1,0:T(8,128)}) custom-call(s32[36]{0:T(128)} %request_ref.1, s32[36]{0:T(128)} %number_ref.1, s32[128]{0:T(128)} %slot_ref.1, s32[128]{0:T(128)} %length_ref.1, bf16[2,16,4,16,128]{4,3,2,1,0:T(8,128)(2,1)} %bitcast.14, bf16[36,1,256,128]{3,2,1,0:T(8,128)(2,1)} %k_ref.1, ...), custom_call_target="tpu_custom_call" | custom-call | tf_op jit(solution)/shard_map/paged_attention/pallas_call | solution.py:90
  44.8 88.7 %second_half.1 = (bf16[32,5120]{1,0:T(8,128)(2,1)}, bf16[32,5120]{1,0:T(8,128)(2,1)}) custom-call(bf16[16,8,16,128]{3,2,1,0:T(8,128)(2,1)} %bitcast.18, f32[16,8,128]{2,1,0:T(8,128)} %bitcast.21, f32[8,16,128]{2,1,0:T(8,128)} %copy-done.5, f32[8,128]{1,0:T(8,128)} %copy-done.7, bf16[32,5120]{1,0:T(8,128)(2,1)} %bitcast.12, f32[40,128]{1,0:T(8,128)} %bitcast.22, ...), custom_call_target="tpu_custom_call" | custom-call | tf_op jit(solution)/shard_map/second_half/pallas_call | solution.py:739
  133.5 1.7 %copy.20 = bf16[4,8,5120]{2,1,0:T(8,128)(2,1)} copy(bf16[4,8,5120]{2,1,0:T(8,128)(2,1)} %bitcast.20) | data formatting | bytes 655360
  135.2 1.7 %copy.21 = bf16[4,8,5120]{2,1,0:T(8,128)(2,1)} copy(bf16[4,8,5120]{2,1,0:T(8,128)(2,1)} %bitcast.19) | data formatting | bytes 655360
  (3 shorter events, 0.0 us)
Async XLA Ops:
  0.7 2.5 %copy-start = (bf16[5120,512]{1,0:T(8,128)(2,1)S(1)}, bf16[5120,512]{1,0:T(8,128)(2,1)}, u32[]{:S(2)}) copy-start(bf16[5120,512]{1,0:T(8,128)(2,1)} %wq_hbm.1) | copy-start | bytes 15728644
  3.2 1.3 copy-start.1
  4.5 1.3 copy-start.2
  5.8 1.0 copy-start.3
  6.8 0.7 copy-start.6
  7.5 0.7 copy-start.8
  8.2 0.7 copy-start.9
  30.0 0.8 copy-start.4
  30.8 0.6 copy-start.5
  31.4 0.6 copy-start.7

commit v4 on v3

--- a/solution.py
+++ b/solution.py
@@ -205,7 +205,7 @@
         self.wire, self.place, self.buf = wire, place, buf
         self.a, self.b, self.c = axes
         self.slots_a = [wire.slot() for _ in range(3)]
-        self.slots_b = [wire.slot() for _ in range(4)]
+        self.slots_b = [wire.slot() for _ in range(3)]
         self.slots_c = [[wire.slot() for _ in range(4)] for _ in range(4)]
         self.slots_p = [[wire.slot() for _ in range(4)] for _ in range(4)]
 
@@ -246,26 +246,13 @@
         for j in (1, 3, 2):
             self.wire.recv(self.slots_a[j - 1], self.block(-j), self.place.device(self.a, -j))
         mine = self.group(0, 0)
-        self.wire.send(self.slots_b[0], mine, mine, self.place.device(self.b, 1))
-        self.wire.send(self.slots_b[1], mine, mine, self.place.device(self.b, -1))
+        for j in (2, 1, 3):
+            self.wire.send(self.slots_b[j - 1], mine, mine, self.place.device(self.b, j))
         self.spread(0)
 
-    def plane_near(self):
-        place, wire = self.place, self.wire
-        wire.recv(self.slots_b[0], self.group(-1, 0), place.device(self.b, -1))
-        part = self.half(-1, 0, 0)
-        wire.send(self.slots_b[2], part, part, place.device(self.b, 1))
-        wire.recv(self.slots_b[1], self.group(1, 0), place.device(self.b, 1))
-        part = self.half(1, 0, 1)
-        wire.send(self.slots_b[3], part, part, place.device(self.b, -1))
-        self.spread(3)
-        self.spread(1)
-
-    def plane_far(self):
-        place, wire = self.place, self.wire
-        wire.recv(self.slots_b[2], self.half(2, 0, 0), place.device(self.b, -1))
-        wire.recv(self.slots_b[3], self.half(2, 0, 1), place.device(self.b, 1))
-        self.spread(2)
+    def plane(self, j):
+        self.wire.recv(self.slots_b[j - 1], self.group(-j, 0), self.place.device(self.b, -j))
+        self.spread(4 - j)
 
     def space_near(self, db):
         place, wire = self.place, self.wire
@@ -340,7 +327,7 @@
 
 
 def slots_needed():
-    return 30 + 7 + 3 * (3 + 4 + 16 + 16) + 12 + 3 * (6 + 6 + 3) + 7
+    return 30 + 7 + 3 * (3 + 3 + 16 + 16) + 12 + 3 * (6 + 3 + 3) + 7
 
 
 def block_kernel(
@@ -383,9 +370,6 @@
     q0,
     q1,
     q2,
-    rb0,
-    rb1,
-    rb2,
     nb0,
     nb1,
     nb2,
@@ -501,13 +485,10 @@
         g.open()
     for g in gathers:
         g.line()
-    for g in gathers:
-        g.plane_near()
-    for g in gathers:
-        g.space_near(0)
-    for g in gathers:
-        g.plane_far()
-    for db in (3, 1, 2):
+    for j in (1, 3, 2):
+        for g in gathers:
+            g.plane(j)
+    for db in (0, 3, 1, 2):
         for g in gathers:
             g.space_near(db)
     for db in (0, 3, 1, 2):
@@ -604,7 +585,7 @@
         lax.fori_loop(0, 4, own_body, 0)
 
     rcs, ncs, qs = (rc0, rc1, rc2), (nc0, nc1, nc2), (q0, q1, q2)
-    rbs, nbs, tas, ras = (rb0, rb1, rb2), (nb0, nb1, nb2), (ta0, ta1, ta2), (ra0, ra1, ra2)
+    nbs, tas, ras = (nb0, nb1, nb2), (ta0, ta1, ta2), (ra0, ra1, ra2)
 
     def piece_c(k):
         def view(d, half):
@@ -613,19 +594,10 @@
 
         return view
 
-    def piece_b(k):
-        def view(d, half):
-            at = place.shifted(AXES[k][1], d)
-            return qs[k].at[at, pl.ds(2 * half, 2)]
-
-        return view
-
     along_c = [
         Scatter(wire, place, AXES[k][2], piece_c(k), rcs[k], ncs[k]) for k in range(3)
     ]
-    along_b = [
-        Scatter(wire, place, AXES[k][1], piece_b(k), rbs[k], nbs[k]) for k in range(3)
-    ]
+    slots_b = [[wire.slot() for _ in range(3)] for _ in range(3)]
     slots_a = [[wire.slot() for _ in range(3)] for _ in range(3)]
     for s in along_c:
         s.open()
@@ -643,16 +615,23 @@
             return carry
 
         lax.fori_loop(0, 4, sum_c, 0)
-        along_b[k].open()
-    for s in along_b:
-        s.pass_on(2)
-    for k, s in enumerate(along_b):
-        s.close()
-        at = place.at[AXES[k][1]]
+        axis = AXES[k][1]
+        for j in (2, 1, 3):
+            wire.send(
+                slots_b[k][j - 1],
+                qs[k].at[place.shifted(axis, j)],
+                nbs[k].at[j - 1],
+                place.device(axis, j),
+            )
+    for k in range(3):
+        axis = AXES[k][1]
+        at = place.at[axis]
+        for j in (1, 3, 2):
+            wire.recv(slots_b[k][j - 1], nbs[k].at[j - 1], place.device(axis, -j))
         for a in range(4):
             v = qs[k][at, a].astype(jnp.float32)
-            v = v + nbs[k][0, a // 2, a % 2].astype(jnp.float32)
-            v = v + nbs[k][1, a // 2, a % 2].astype(jnp.float32)
+            for j in range(3):
+                v = v + nbs[k][j, a].astype(jnp.float32)
             tas[k][a] = v.astype(jnp.bfloat16)
         for j in (2, 1, 3):
             axis = AXES[k][0]
@@ -720,8 +699,7 @@
         *each(2, 2, 4),
         *each(2, 2, 2, 4),
         *each(4, 4),
-        *each(2, 2),
-        *each(2, 2, 2),
+        *each(3, 4),
         *each(4),
         *each(3),
         vm((rows, cols), bf),
@@ -743,7 +721,7 @@
         out_specs=[whole, whole],
         scratch_shapes=scratch,
         compiler_params=pltpu.CompilerParams(
-            collective_id=1, has_side_effects=True, vmem_limit_bytes=60 * 1024 * 1024
+            collective_id=1, has_side_effects=True, vmem_limit_bytes=63 * 1024 * 1024
         ),
         name="second_half",
     )(part, lse, fresh, fresh_lse, x, gain, w_output, w_gate, w_up, w_down)
@@ -943,7 +921,7 @@
             pltpu.SemaphoreType.DMA((14,)),
         ],
         compiler_params=pltpu.CompilerParams(
-            collective_id=2, has_side_effects=True, vmem_limit_bytes=40 * 1024 * 1024
+            collective_id=2, has_side_effects=True, vmem_limit_bytes=63 * 1024 * 1024
         ),
         name="first_half",
     )(x, gain[None, :], freq, slot[None, :], lengths[None, :], w_query, w_key, w_value)

time: 137 us -> 123 us (0.90)
  local copies, waits for them, and re-layouts: 13.6 us -> 3.44 us
  Pallas kernels: 123 us -> 118 us
    unnamed x22 -> x2, local copies, waits for them, and re-layouts: 13.6 us -> 3.44 us
    pallas_call x1, Pallas kernels: 88.7 us -> 85.8 us  [second_half(): pl.pallas_call(functools.partial(block_kernel, widths), out_shape=[out, o...]
    pallas_call x1, Pallas kernels: 21.1 us -> 19 us  [first_half(): pl.pallas_call(project_kernel, out_shape=[jax.ShapeDtypeStruct((2, 4, 4,...]
where the time goes in v4:
time: 123 us; the launch traced here: 122 us
  Pallas kernels  118 us (96%)
  local copies, waits for them, and re-layouts  3.44 us (3%)
    pallas_call x1, Pallas kernels, second_half(): pl.pallas_call(functools.partial(block_kernel, widths), out_shape=[out, o...  85.8 us
    pallas_call x1, Pallas kernels, first_half(): pl.pallas_call(project_kernel, out_shape=[jax.ShapeDtypeStruct((2, 4, 4,...  19 us
    pallas_call x1, Pallas kernels, paged_attention(): pl.pallas_call(functools.partial(paged_kernel, pages), grid_spec=pltpu.Pr...  12.8 us
    unnamed x2, local copies, waits for them, and re-layouts  3.44 us

profile of v4, /device:TPU:1, one launch (start us, length us, event | category | flops | bytes accessed | tf_op | source)
XLA Modules:
  0.0 122.2 jit_solution(12220795511868033387)
XLA Ops:
  0.6 0.6 maximum_bitcast_fusion.freq_ref
  1.2 19.0 %first_half.1 = (bf16[2,4,4,4,16,128]{5,4,3,2,1,0:T(8,128)(2,1)}, f32[8,16,128]{2,1,0:T(8,128)}, f32[8,128]{1,0:T(8,128)}) custom-call(bf16[32,5120]{1,0:T(8,128)(2,1)} %bitcast.12, f32[1,5120]{1,0:T(1,128)} %bitcast.19, f32[1,128]{1,0:T(1,128)} %maximum_bitcast_fusion.freq_ref, s32[1,128]{1,0:T(1,128)} %bitcast.21, s32[1,128]{1,0:T(1,128)} %bitcast.22, ...), custom_call_target="tpu_custom_call" | custom-call | tf_op jit(solution)/shard_map/first_half/pallas_call | solution.py:905
  20.2 12.8 %paged_attention.1 = (bf16[128,16,128]{2,1,0:T(8,128)(2,1)}, f32[128,128]{1,0:T(8,128)}) custom-call(s32[36]{0:T(128)} %request_ref.1, s32[36]{0:T(128)} %number_ref.1, s32[128]{0:T(128)} %slot_ref.1, s32[128]{0:T(128)} %length_ref.1, bf16[2,16,4,16,128]{4,3,2,1,0:T(8,128)(2,1)} %bitcast.14, bf16[36,1,256,128]{3,2,1,0:T(8,128)(2,1)} %k_ref.1, ...), custom_call_target="tpu_custom_call" | custom-call | tf_op jit(solution)/shard_map/paged_attention/pallas_call | solution.py:90
  33.0 85.8 %second_half.1 = (bf16[32,5120]{1,0:T(8,128)(2,1)}, bf16[32,5120]{1,0:T(8,128)(2,1)}) custom-call(bf16[16,8,16,128]{3,2,1,0:T(8,128)(2,1)} %bitcast.15, f32[16,8,128]{2,1,0:T(8,128)} %bitcast.18, f32[8,16,128]{2,1,0:T(8,128)} %get-tuple-element.12.fresh_ref, f32[8,128]{1,0:T(8,128)} %get-tuple-element.13.fresh_lse_ref, bf16[32,5120]{1,0:T(8,128)(2,1)} %bitcast.13, ...), custom_call_target="tpu_custom_call" | custom-call | tf_op jit(solution)/shard_map/second_half/pallas_call | solution.py:717
  118.8 1.7 %copy.20 = bf16[4,8,5120]{2,1,0:T(8,128)(2,1)} copy(bf16[4,8,5120]{2,1,0:T(8,128)(2,1)} %bitcast.17) | data formatting | bytes 655360
  120.5 1.7 %copy.21 = bf16[4,8,5120]{2,1,0:T(8,128)(2,1)} copy(bf16[4,8,5120]{2,1,0:T(8,128)(2,1)} %bitcast.16) | data formatting | bytes 655360
  (1 shorter events, 0.0 us)

commit v5 on v4

--- a/solution.py
+++ b/solution.py
@@ -60,18 +60,16 @@
 
     @pl.when(step == pl.num_programs(0) - 1)
     def _():
-        l = l_s[...]
-        safe = jnp.where(l > 0.0, l, 1.0)
-        o_ref[...] = (acc_s[...] / safe).astype(o_ref.dtype)
-        lse = jnp.where(l > 0.0, m_s[...] + jnp.log(safe), masked_low)
-        lse_ref[...] = compact(lse)
-
-
-def compact(values):
-    eye = lax.broadcasted_iota(jnp.int32, values.shape, 1) == lax.broadcasted_iota(
-        jnp.int32, values.shape, 2
-    )
-    return jnp.sum(jnp.where(eye, values, 0.0), axis=1)
+        o_ref[...] = acc_s[...].astype(o_ref.dtype)
+        lse_ref[...] = compact(m_s[...], l_s[...])
+
+
+def compact(tops, sums):
+    row = lax.broadcasted_iota(jnp.int32, tops.shape, 1)
+    lane = lax.broadcasted_iota(jnp.int32, tops.shape, 2)
+    count = tops.shape[1]
+    picked = jnp.where(lane == row, tops, jnp.where(lane == row + count, sums, 0.0))
+    return jnp.sum(picked, axis=1)
 
 
 def expand(values, count):
@@ -85,7 +83,7 @@
     group, dim = queries.shape[-2:]
     total = slot.shape[0]
     count, _, length, _ = keys.shape
-    pages = next(n for n in (6, 4, 3, 2, 1) if count % n == 0)
+    pages = next(n for n in (12, 9, 6, 4, 3, 2, 1) if count % n == 0)
     paged = pl.BlockSpec((pages, None, length, dim), lambda i, *_: (i, 0, 0, 0))
     return pl.pallas_call(
         functools.partial(paged_kernel, pages),
@@ -441,12 +439,15 @@
     count = part_ref.shape[2]
     sums = [lses[n] for n in range(15)] + [lse_ref[place.s], fresh_lse_ref[...]]
     top = functools.reduce(jnp.maximum, sums)
-    sums = [jnp.exp(v - top) for v in sums]
-    whole = functools.reduce(jnp.add, sums)
-    attention = fresh_ref[...] * expand(sums[16] / whole, count)
+    shares = [jnp.exp(v - top) for v in sums]
+    totals = [pltpu.roll(v, v.shape[1] - count, 1) for v in sums]
+    whole = functools.reduce(jnp.add, [w * v for w, v in zip(shares, totals)])
+    used = lax.broadcasted_iota(jnp.int32, top.shape, 1) < count
+    shares = [jnp.where(used, w / jnp.where(used, whole, 1.0), 0.0) for w in shares]
+    attention = fresh_ref[...] * expand(shares[16], count)
     for n in range(15):
-        attention += parts[n].astype(jnp.float32) * expand(sums[n] / whole, count)
-    attention += part_ref[place.s].astype(jnp.float32) * expand(sums[15] / whole, count)
+        attention += parts[n].astype(jnp.float32) * expand(shares[n], count)
+    attention += part_ref[place.s].astype(jnp.float32) * expand(shares[15], count)
     att32[...] = attention
     per_step = count // STEPS
     heads = jnp.concatenate(
@@ -732,16 +733,13 @@
         self.wire, self.place, self.buf = wire, place, buf
         self.a, self.b = axes
         self.slots_a = [wire.slot() for _ in range(3)]
-        self.slots_b = [wire.slot() for _ in range(4)]
+        self.slots_b = [wire.slot() for _ in range(3)]
 
     def cut(self, b, a):
         return self.buf.at[b, a] if self.b == "z" else self.buf.at[a, b]
 
     def block(self, da):
         return self.cut(self.place.at[self.b], self.place.shifted(self.a, da))
-
-    def half(self, db, which):
-        return self.cut(self.place.shifted(self.b, db), pl.ds(2 * which, 2))
 
     def group(self, db):
         return self.cut(self.place.shifted(self.b, db), pl.ds(0, 4))
@@ -755,22 +753,12 @@
         for j in (1, 3, 2):
             self.wire.recv(self.slots_a[j - 1], self.block(-j), self.place.device(self.a, -j))
         mine = self.group(0)
-        self.wire.send(self.slots_b[0], mine, mine, self.place.device(self.b, 1))
-        self.wire.send(self.slots_b[1], mine, mine, self.place.device(self.b, -1))
-
-    def near(self):
-        place, wire = self.place, self.wire
-        wire.recv(self.slots_b[0], self.group(-1), place.device(self.b, -1))
-        part = self.half(-1, 0)
-        wire.send(self.slots_b[2], part, part, place.device(self.b, 1))
-        wire.recv(self.slots_b[1], self.group(1), place.device(self.b, 1))
-        part = self.half(1, 1)
-        wire.send(self.slots_b[3], part, part, place.device(self.b, -1))
-
-    def far(self):
-        place, wire = self.place, self.wire
-        wire.recv(self.slots_b[2], self.half(2, 0), place.device(self.b, -1))
-        wire.recv(self.slots_b[3], self.half(2, 1), place.device(self.b, 1))
+        for j in (2, 1, 3):
+            self.wire.send(self.slots_b[j - 1], mine, mine, self.place.device(self.b, j))
+
+    def plane(self):
+        for j in (1, 3, 2):
+            self.wire.recv(self.slots_b[j - 1], self.group(-j), self.place.device(self.b, -j))
 
 
 def project_kernel(
@@ -878,16 +866,17 @@
     w = jnp.where(allowed, jnp.exp(s - top), 0.0)
     total = jnp.sum(w, axis=-1, keepdims=True)
     acc = jnp.dot(w.astype(jnp.bfloat16), new_v, preferred_element_type=jnp.float32)
-    fresh_ref[...] = (acc / total).reshape(own, count, dim)
-    lse = jnp.broadcast_to(top + jnp.log(total), (own * count, dim))
-    fresh_lse_ref[...] = compact(lse.reshape(own, count, dim))
+    fresh_ref[...] = acc.reshape(own, count, dim)
+    shape = (own, count, dim)
+    fresh_lse_ref[...] = compact(
+        jnp.broadcast_to(top, (own * count, dim)).reshape(shape),
+        jnp.broadcast_to(total, (own * count, dim)).reshape(shape),
+    )
 
     for g in gathers:
         g.line()
     for g in gathers:
-        g.near()
-    for g in gathers:
-        g.far()
+        g.plane()
     wire.drain()
 
 
@@ -917,14 +906,24 @@
             vm(w_value.shape, bf),
             vm((own, count, dim), f32),
             pltpu.SemaphoreType.DMA((8, 3)),
-            pltpu.SemaphoreType.DMA((14,)),
-            pltpu.SemaphoreType.DMA((14,)),
+            pltpu.SemaphoreType.DMA((12,)),
+            pltpu.SemaphoreType.DMA((12,)),
         ],
         compiler_params=pltpu.CompilerParams(
             collective_id=2, has_side_effects=True, vmem_limit_bytes=63 * 1024 * 1024
         ),
         name="first_half",
     )(x, gain[None, :], freq, slot[None, :], lengths[None, :], w_query, w_key, w_value)
+
+
+def finish_kernel(a_ref, b_ref, c_ref, d_ref):
+    c_ref[...] = a_ref[...].reshape(c_ref.shape)
+    d_ref[...] = b_ref[...].reshape(d_ref.shape)
+
+
+def finish(attended, layer_out, shape):
+    out = jax.ShapeDtypeStruct(shape, attended.dtype)
+    return pl.pallas_call(finish_kernel, out_shape=[out, out], name="finish")(attended, layer_out)
 
 
 def local(
@@ -975,7 +974,7 @@
         w_down,
     )
     shape = (steps, row_count, width)
-    return attended.reshape(shape), layer_out.reshape(shape)
+    return tuple(finish(attended, layer_out, shape))
 
 
 def solution(mesh):

time: 123 us -> 118 us (0.959)
  local copies, waits for them, and re-layouts: 3.44 us -> 0 us
    unnamed x2 -> x0, local copies, waits for them, and re-layouts: 3.44 us -> none
    pallas_call x1, Pallas kernels: 19 us -> 16.7 us  [first_half(): pl.pallas_call(project_kernel, out_shape=[jax.ShapeDtypeStruct((2, 4, 4,...]
    pallas_call x0 -> x1, Pallas kernels: none -> 1.93 us  [finish(): pl.pallas_call(finish_kernel, out_shape=[out, out], name='finish')]
where the time goes in v5:
time: 118 us
  Pallas kernels  117 us (99%)
    pallas_call x1, Pallas kernels, second_half(): pl.pallas_call(functools.partial(block_kernel, widths), out_shape=[out, o...  85.5 us
    pallas_call x1, Pallas kernels, first_half(): pl.pallas_call(project_kernel, out_shape=[jax.ShapeDtypeStruct((2, 4, 4,...  16.7 us
    pallas_call x1, Pallas kernels, paged_attention(): pl.pallas_call(functools.partial(paged_kernel, pages), grid_spec=pltpu.Pr...  12.4 us

profile of v5, /device:TPU:1, one launch (start us, length us, event | category | flops | bytes accessed | tf_op | source)
XLA Modules:
  0.0 117.8 jit_solution(505752019650946487)
XLA Ops:
  0.6 0.6 maximum_bitcast_fusion.freq_ref
  1.2 16.7 %first_half.1 = (bf16[2,4,4,4,16,128]{5,4,3,2,1,0:T(8,128)(2,1)}, f32[8,16,128]{2,1,0:T(8,128)}, f32[8,128]{1,0:T(8,128)}) custom-call(bf16[32,5120]{1,0:T(8,128)(2,1)} %bitcast.10, f32[1,5120]{1,0:T(1,128)} %bitcast.15, f32[1,128]{1,0:T(1,128)} %maximum_bitcast_fusion.freq_ref, s32[1,128]{1,0:T(1,128)} %bitcast.17, s32[1,128]{1,0:T(1,128)} %bitcast.18, ...), custom_call_target="tpu_custom_call" | custom-call | tf_op jit(solution)/shard_map/first_half/pallas_call | solution.py:894
  18.0 12.4 %paged_attention.1 = (bf16[128,16,128]{2,1,0:T(8,128)(2,1)}, f32[128,128]{1,0:T(8,128)}) custom-call(s32[36]{0:T(128)} %request_ref.1, s32[36]{0:T(128)} %number_ref.1, s32[128]{0:T(128)} %slot_ref.1, s32[128]{0:T(128)} %length_ref.1, bf16[2,16,4,16,128]{4,3,2,1,0:T(8,128)(2,1)} %bitcast.12, bf16[36,1,256,128]{3,2,1,0:T(8,128)(2,1)} %k_ref.1, ...), custom_call_target="tpu_custom_call" | custom-call | tf_op jit(solution)/shard_map/paged_attention/pallas_call | solution.py:88
  30.3 85.5 %second_half.1 = (bf16[32,5120]{1,0:T(8,128)(2,1)}, bf16[32,5120]{1,0:T(8,128)(2,1)}) custom-call(bf16[16,8,16,128]{3,2,1,0:T(8,128)(2,1)} %bitcast.13, f32[16,8,128]{2,1,0:T(8,128)} %bitcast.14, f32[8,16,128]{2,1,0:T(8,128)} %get-tuple-element.12.fresh_ref, f32[8,128]{1,0:T(8,128)} %get-tuple-element.13.fresh_lse_ref, bf16[32,5120]{1,0:T(8,128)(2,1)} %bitcast.11, ...), custom_call_target="tpu_custom_call" | custom-call | tf_op jit(solution)/shard_map/second_half/pallas_call | solution.py:718
  115.8 1.9 %finish.1 = (bf16[4,8,5120]{2,1,0:T(8,128)(2,1)}, bf16[4,8,5120]{2,1,0:T(8,128)(2,1)}) custom-call(bf16[32,5120]{1,0:T(8,128)(2,1)} %get-tuple-element.14.a_ref, bf16[32,5120]{1,0:T(8,128)(2,1)} %get-tuple-element.15.b_ref), custom_call_target="tpu_custom_call" | custom-call | tf_op jit(solution)/shard_map/finish/pallas_call | solution.py:926
  (1 shorter events, 0.0 us)

commit v6 on v5

--- a/solution.py
+++ b/solution.py
@@ -271,15 +271,12 @@
         wire.recv(slots[3], self.half(db, 2, 1), place.device(self.c, 1))
         self.over(db, 2)
 
-    def other_core(self):
+    def other_core(self, dc):
         place = self.place
         for db in (0, 3, 1, 2):
-            for dc in (0, 3, 1, 2):
-                self.wire.recv(
-                    self.slots_p[db][dc],
-                    self.group(db, dc, 1 - place.core),
-                    place.device(flip=True),
-                )
+            self.wire.recv(
+                self.slots_p[db][dc], self.group(db, dc, 1 - place.core), place.device(flip=True)
+            )
 
 
 def add_into(dst, src, count):
@@ -489,51 +486,82 @@
     for j in (1, 3, 2):
         for g in gathers:
             g.plane(j)
+
+    acc[...] = jnp.zeros_like(acc)
+    squares[...] = jnp.zeros_like(squares)
+
+    def squared(v):
+        total = None
+        for n in range(v.shape[-1] // 128):
+            f = v[:, n * 128 : n * 128 + 128].astype(jnp.float32)
+            total = f * f if total is None else total + f * f
+        return total
+
+    def product(v, w):
+        return jnp.dot(v, w, preferred_element_type=jnp.float32)
+
+    def use_slab(dc, c):
+        z, y1, x = place.shifted("z", dc), place.shifted("y", dc), place.shifted("x", dc)
+
+        def first_body(y, carry):
+            v = g0[c, z, :, y].reshape(128, widths[0])
+            d = product(v, wgu[columns(y * 2 + c, 0, widths[0]), :])
+            acc[z] += d.reshape(4, 32, 2 * ff)
+            squares[z] += squared(v).reshape(4, 32, 128)
+            return carry
+
+        lax.fori_loop(0, 4, first_body, 0)
+
+        def middle_body(i, carry):
+            v = g1[c, y1, i].reshape(128, widths[1])
+            d = product(v, wgu[columns(y1 * 2 + c, starts[1], widths[1]), :])
+            acc[i] += d.reshape(4, 32, 2 * ff)
+            squares[i] += squared(v).reshape(4, 32, 128)
+            return carry
+
+        lax.fori_loop(0, 4, middle_body, 0)
+
+        def last_body(i, carry):
+            vs = [g2[c, x, i * 2 + n].reshape(128, widths[2]) for n in range(2)]
+            ws = [
+                wgu[columns((i * 2 + n) * 2 + c, starts[2], widths[2]), :] for n in range(2)
+            ]
+            v = jnp.concatenate(vs, axis=1)
+            d = product(v, jnp.concatenate(ws, axis=0))
+            acc[:, x] += d.reshape(4, 32, 2 * ff)
+            squares[:, x] += squared(v).reshape(4, 32, 128)
+            return carry
+
+        lax.fori_loop(0, 2, last_body, 0)
+
+    use_slab(0, core)
     for db in (0, 3, 1, 2):
         for g in gathers:
             g.space_near(db)
+    use_slab(3, core)
+    use_slab(1, core)
+    for g in gathers:
+        g.other_core(0)
+    use_slab(0, 1 - core)
     for db in (0, 3, 1, 2):
         for g in gathers:
             g.space_far(db)
+    for dc in (3, 1):
+        for g in gathers:
+            g.other_core(dc)
+        use_slab(dc, 1 - core)
+    use_slab(2, core)
     for g in gathers:
-        g.other_core()
-
-    acc[...] = jnp.zeros_like(acc)
-    squares[...] = jnp.zeros_like(squares)
-
-    def rows_of(k, c, y):
-        if k == 0:
-            v = gs[0][c, :, :, y]
-        elif k == 1:
-            v = gs[1][c, y]
-        else:
-            v = jnp.stack(
-                [jnp.stack([gs[2][c, x, y, z] for x in range(4)]) for z in range(4)]
-            )
-        return v.reshape(512, v.shape[-1])
-
-    def up_body(i, carry):
-        c, y = i // 4, i % 4
-        tt = y * 2 + c
-        for k in range(3):
-            v = rows_of(k, c, y)
-            w = wgu[columns(tt, starts[k], widths[k]), :]
-            acc[...] += jnp.dot(v, w, preferred_element_type=jnp.float32)
-            sq = None
-            for n in range(widths[k] // 128):
-                f = v[:, n * 128 : n * 128 + 128].astype(jnp.float32)
-                sq = f * f if sq is None else sq + f * f
-            squares[...] += sq
-        return carry
-
-    lax.fori_loop(0, 8, up_body, 0)
+        g.other_core(2)
+    use_slab(2, 1 - core)
 
     def act_body(i, carry):
         rows = pl.ds(pl.multiple_of(i * 128, 128), 128)
-        mean = jnp.sum(squares[rows, :], axis=-1, keepdims=True) / (8 * cols)
+        mean = jnp.sum(squares[i].reshape(128, 128), axis=-1, keepdims=True) / (8 * cols)
         r = lax.rsqrt(mean + norm_eps)
-        gate = acc[rows, :ff] * r
-        up = acc[rows, ff:] * r
+        both = acc[i].reshape(128, 2 * ff) * r
+        gate = both[:, :ff]
+        up = both[:, ff:]
         act[rows, :] = (gate / (1.0 + jnp.exp(-gate)) * up).astype(act.dtype)
         return carry
 
@@ -692,8 +720,8 @@
         vm((7, rows, cols), bf),
         vm((7, rows, cols), bf),
         *each(2, 4, 4, 4),
-        vm((512, 2 * ff), f32),
-        vm((512, 128), f32),
+        vm((4, 4, 32, 2 * ff), f32),
+        vm((4, 4, 32, 128), f32),
         vm((512, ff), bf),
         *each(2, 4, 4, 4),
         *each(4, 4, 4),

time: 118 us -> 120 us (1.017)
  Pallas kernels: 117 us -> 119 us
    pallas_call x1, Pallas kernels: 85.5 us -> 88 us  [second_half(): pl.pallas_call(functools.partial(block_kernel, widths), out_shape=[out, o...]
where the time goes in v6:
time: 120 us
  Pallas kernels  119 us (99%)
    pallas_call x1, Pallas kernels, second_half(): pl.pallas_call(functools.partial(block_kernel, widths), out_shape=[out, o...  88 us
    pallas_call x1, Pallas kernels, first_half(): pl.pallas_call(project_kernel, out_shape=[jax.ShapeDtypeStruct((2, 4, 4,...  16.7 us
    pallas_call x1, Pallas kernels, paged_attention(): pl.pallas_call(functools.partial(paged_kernel, pages), grid_spec=pltpu.Pr...  12.4 us

profile of v6, /device:TPU:1, one launch (start us, length us, event | category | flops | bytes accessed | tf_op | source)
XLA Modules:
  0.0 120.2 jit_solution(6242574048446408478)
XLA Ops:
  0.6 0.6 maximum_bitcast_fusion.freq_ref
  1.2 16.7 %first_half.1 = (bf16[2,4,4,4,16,128]{5,4,3,2,1,0:T(8,128)(2,1)}, f32[8,16,128]{2,1,0:T(8,128)}, f32[8,128]{1,0:T(8,128)}) custom-call(bf16[32,5120]{1,0:T(8,128)(2,1)} %bitcast.10, f32[1,5120]{1,0:T(1,128)} %bitcast.15, f32[1,128]{1,0:T(1,128)} %maximum_bitcast_fusion.freq_ref, s32[1,128]{1,0:T(1,128)} %bitcast.17, s32[1,128]{1,0:T(1,128)} %bitcast.18, ...), custom_call_target="tpu_custom_call" | custom-call | tf_op jit(solution)/shard_map/first_half/pallas_call | solution.py:922
  18.0 12.4 %paged_attention.1 = (bf16[128,16,128]{2,1,0:T(8,128)(2,1)}, f32[128,128]{1,0:T(8,128)}) custom-call(s32[36]{0:T(128)} %request_ref.1, s32[36]{0:T(128)} %number_ref.1, s32[128]{0:T(128)} %slot_ref.1, s32[128]{0:T(128)} %length_ref.1, bf16[2,16,4,16,128]{4,3,2,1,0:T(8,128)(2,1)} %bitcast.12, bf16[36,1,256,128]{3,2,1,0:T(8,128)(2,1)} %k_ref.1, ...), custom_call_target="tpu_custom_call" | custom-call | tf_op jit(solution)/shard_map/paged_attention/pallas_call | solution.py:88
  30.3 88.0 %second_half.1 = (bf16[32,5120]{1,0:T(8,128)(2,1)}, bf16[32,5120]{1,0:T(8,128)(2,1)}) custom-call(bf16[16,8,16,128]{3,2,1,0:T(8,128)(2,1)} %bitcast.13, f32[16,8,128]{2,1,0:T(8,128)} %bitcast.14, f32[8,16,128]{2,1,0:T(8,128)} %get-tuple-element.12.fresh_ref, f32[8,128]{1,0:T(8,128)} %get-tuple-element.13.fresh_lse_ref, bf16[32,5120]{1,0:T(8,128)(2,1)} %bitcast.11, ...), custom_call_target="tpu_custom_call" | custom-call | tf_op jit(solution)/shard_map/second_half/pallas_call | solution.py:746
  118.3 1.9 %finish.1 = (bf16[4,8,5120]{2,1,0:T(8,128)(2,1)}, bf16[4,8,5120]{2,1,0:T(8,128)(2,1)}) custom-call(bf16[32,5120]{1,0:T(8,128)(2,1)} %get-tuple-element.14.a_ref, bf16[32,5120]{1,0:T(8,128)(2,1)} %get-tuple-element.15.b_ref), custom_call_target="tpu_custom_call" | custom-call | tf_op jit(solution)/shard_map/finish/pallas_call | solution.py:954
  (1 shorter events, 0.0 us)

commit v7 on v6

--- a/solution.py
+++ b/solution.py
@@ -500,39 +500,14 @@
     def product(v, w):
         return jnp.dot(v, w, preferred_element_type=jnp.float32)
 
+    def take(v, w):
+        acc[...] += product(v, w).reshape(acc.shape)
+        squares[...] += squared(v).reshape(squares.shape)
+
     def use_slab(dc, c):
-        z, y1, x = place.shifted("z", dc), place.shifted("y", dc), place.shifted("x", dc)
-
-        def first_body(y, carry):
-            v = g0[c, z, :, y].reshape(128, widths[0])
-            d = product(v, wgu[columns(y * 2 + c, 0, widths[0]), :])
-            acc[z] += d.reshape(4, 32, 2 * ff)
-            squares[z] += squared(v).reshape(4, 32, 128)
-            return carry
-
-        lax.fori_loop(0, 4, first_body, 0)
-
-        def middle_body(i, carry):
-            v = g1[c, y1, i].reshape(128, widths[1])
-            d = product(v, wgu[columns(y1 * 2 + c, starts[1], widths[1]), :])
-            acc[i] += d.reshape(4, 32, 2 * ff)
-            squares[i] += squared(v).reshape(4, 32, 128)
-            return carry
-
-        lax.fori_loop(0, 4, middle_body, 0)
-
-        def last_body(i, carry):
-            vs = [g2[c, x, i * 2 + n].reshape(128, widths[2]) for n in range(2)]
-            ws = [
-                wgu[columns((i * 2 + n) * 2 + c, starts[2], widths[2]), :] for n in range(2)
-            ]
-            v = jnp.concatenate(vs, axis=1)
-            d = product(v, jnp.concatenate(ws, axis=0))
-            acc[:, x] += d.reshape(4, 32, 2 * ff)
-            squares[:, x] += squared(v).reshape(4, 32, 128)
-            return carry
-
-        lax.fori_loop(0, 2, last_body, 0)
+        y = place.shifted("y", dc)
+        v = g1[c, y].reshape(512, widths[1])
+        take(v, wgu[columns(y * 2 + c, starts[1], widths[1]), :])
 
     use_slab(0, core)
     for db in (0, 3, 1, 2):
@@ -540,20 +515,43 @@
             g.space_near(db)
     use_slab(3, core)
     use_slab(1, core)
-    for g in gathers:
-        g.other_core(0)
+    gathers[1].other_core(0)
     use_slab(0, 1 - core)
     for db in (0, 3, 1, 2):
-        for g in gathers:
+        for g in (gathers[2], gathers[1], gathers[0]):
             g.space_far(db)
     for dc in (3, 1):
-        for g in gathers:
-            g.other_core(dc)
+        gathers[1].other_core(dc)
         use_slab(dc, 1 - core)
     use_slab(2, core)
-    for g in gathers:
-        g.other_core(2)
+    gathers[1].other_core(2)
     use_slab(2, 1 - core)
+    for dc in range(4):
+        gathers[2].other_core(dc)
+
+    def last_body(i, carry):
+        c, half = i // 2, i % 2
+        vs = []
+        ws = []
+        for n in range(2):
+            y = half * 2 + n
+            v = jnp.stack([jnp.stack([g2[c, x, y, z] for x in range(4)]) for z in range(4)])
+            vs.append(v.reshape(512, widths[2]))
+            ws.append(wgu[columns(y * 2 + c, starts[2], widths[2]), :])
+        take(jnp.concatenate(vs, axis=1), jnp.concatenate(ws, axis=0))
+        return carry
+
+    lax.fori_loop(0, 4, last_body, 0)
+    for dc in range(4):
+        gathers[0].other_core(dc)
+
+    def first_body(i, carry):
+        c, y = i // 4, i % 4
+        v = g0[c, :, :, y].reshape(512, widths[0])
+        take(v, wgu[columns(y * 2 + c, 0, widths[0]), :])
+        return carry
+
+    lax.fori_loop(0, 8, first_body, 0)
 
     def act_body(i, carry):
         rows = pl.ds(pl.multiple_of(i * 128, 128), 128)

time: 120 us -> 117 us (0.975)
  Pallas kernels: 119 us -> 116 us
    pallas_call x1, Pallas kernels: 88 us -> 84.5 us  [second_half(): pl.pallas_call(functools.partial(block_kernel, widths), out_shape=[out, o...]
where the time goes in v7:
time: 117 us
  Pallas kernels  116 us (99%)
    pallas_call x1, Pallas kernels, second_half(): pl.pallas_call(functools.partial(block_kernel, widths), out_shape=[out, o...  84.5 us
    pallas_call x1, Pallas kernels, first_half(): pl.pallas_call(project_kernel, out_shape=[jax.ShapeDtypeStruct((2, 4, 4,...  16.7 us
    pallas_call x1, Pallas kernels, paged_attention(): pl.pallas_call(functools.partial(paged_kernel, pages), grid_spec=pltpu.Pr...  12.4 us

profile of v7, /device:TPU:1, one launch (start us, length us, event | category | flops | bytes accessed | tf_op | source)
XLA Modules:
  0.0 116.8 jit_solution(13963360822522503922)
XLA Ops:
  0.6 0.6 maximum_bitcast_fusion.freq_ref
  1.2 16.7 %first_half.1 = (bf16[2,4,4,4,16,128]{5,4,3,2,1,0:T(8,128)(2,1)}, f32[8,16,128]{2,1,0:T(8,128)}, f32[8,128]{1,0:T(8,128)}) custom-call(bf16[32,5120]{1,0:T(8,128)(2,1)} %bitcast.10, f32[1,5120]{1,0:T(1,128)} %bitcast.15, f32[1,128]{1,0:T(1,128)} %maximum_bitcast_fusion.freq_ref, s32[1,128]{1,0:T(1,128)} %bitcast.17, s32[1,128]{1,0:T(1,128)} %bitcast.18, ...), custom_call_target="tpu_custom_call" | custom-call | tf_op jit(solution)/shard_map/first_half/pallas_call | solution.py:920
  18.0 12.4 %paged_attention.1 = (bf16[128,16,128]{2,1,0:T(8,128)(2,1)}, f32[128,128]{1,0:T(8,128)}) custom-call(s32[36]{0:T(128)} %request_ref.1, s32[36]{0:T(128)} %number_ref.1, s32[128]{0:T(128)} %slot_ref.1, s32[128]{0:T(128)} %length_ref.1, bf16[2,16,4,16,128]{4,3,2,1,0:T(8,128)(2,1)} %bitcast.12, bf16[36,1,256,128]{3,2,1,0:T(8,128)(2,1)} %k_ref.1, ...), custom_call_target="tpu_custom_call" | custom-call | tf_op jit(solution)/shard_map/paged_attention/pallas_call | solution.py:88
  30.3 84.5 %second_half.1 = (bf16[32,5120]{1,0:T(8,128)(2,1)}, bf16[32,5120]{1,0:T(8,128)(2,1)}) custom-call(bf16[16,8,16,128]{3,2,1,0:T(8,128)(2,1)} %bitcast.13, f32[16,8,128]{2,1,0:T(8,128)} %bitcast.14, f32[8,16,128]{2,1,0:T(8,128)} %get-tuple-element.12.fresh_ref, f32[8,128]{1,0:T(8,128)} %get-tuple-element.13.fresh_lse_ref, bf16[32,5120]{1,0:T(8,128)(2,1)} %bitcast.11, ...), custom_call_target="tpu_custom_call" | custom-call | tf_op jit(solution)/shard_map/second_half/pallas_call | solution.py:744
  114.8 1.9 %finish.1 = (bf16[4,8,5120]{2,1,0:T(8,128)(2,1)}, bf16[4,8,5120]{2,1,0:T(8,128)(2,1)}) custom-call(bf16[32,5120]{1,0:T(8,128)(2,1)} %get-tuple-element.14.a_ref, bf16[32,5120]{1,0:T(8,128)(2,1)} %get-tuple-element.15.b_ref), custom_call_target="tpu_custom_call" | custom-call | tf_op jit(solution)/shard_map/finish/pallas_call | solution.py:952
  (1 shorter events, 0.0 us)

commit v8 on v7

--- a/solution.py
+++ b/solution.py
@@ -2,6 +2,7 @@
 
 import jax
 import jax.numpy as jnp
+import numpy as np
 from jax import lax
 from jax.experimental import pallas as pl
 from jax.experimental.pallas import tpu as pltpu
@@ -246,7 +247,6 @@
         mine = self.group(0, 0)
         for j in (2, 1, 3):
             self.wire.send(self.slots_b[j - 1], mine, mine, self.place.device(self.b, j))
-        self.spread(0)
 
     def plane(self, j):
         self.wire.recv(self.slots_b[j - 1], self.group(-j, 0), self.place.device(self.b, -j))
@@ -486,6 +486,8 @@
     for j in (1, 3, 2):
         for g in gathers:
             g.plane(j)
+            if j == 1:
+                g.spread(0)
 
     acc[...] = jnp.zeros_like(acc)
     squares[...] = jnp.zeros_like(squares)
@@ -912,9 +914,9 @@
     count = STEPS * w_query.shape[1] // dim
     own = rows // STEPS
     bf, f32, vm = jnp.bfloat16, jnp.float32, pltpu.VMEM
-    exponent = jnp.arange(dim // 2, dtype=f32) * (2.0 / dim)
-    freq = rope_theta ** (-exponent)
-    freq = jnp.concatenate([freq, freq])[None, :]
+    exponent = np.arange(dim // 2, dtype=np.float32) * np.float32(2.0 / dim)
+    freq = (rope_theta ** -exponent.astype(np.float64)).astype(np.float32)
+    freq = jnp.asarray(np.concatenate([freq, freq])[None, :])
     whole = pl.BlockSpec(memory_space=pltpu.VMEM)
     hbm = pl.BlockSpec(memory_space=pl.ANY)
     return pl.pallas_call(

time: 117 us -> 116 us (level)
  no operation moved by 1% of the time
where the time goes in v8:
time: 116 us
  Pallas kernels  115 us (99%)
    pallas_call x1, Pallas kernels, second_half(): pl.pallas_call(functools.partial(block_kernel, widths), out_shape=[out, o...  84 us
    pallas_call x1, Pallas kernels, first_half(): pl.pallas_call(project_kernel, out_shape=[jax.ShapeDtypeStruct((2, 4, 4,...  16.8 us
    pallas_call x1, Pallas kernels, paged_attention(): pl.pallas_call(functools.partial(paged_kernel, pages), grid_spec=pltpu.Pr...  12.4 us

profile of v8, /device:TPU:1, one launch (start us, length us, event | category | flops | bytes accessed | tf_op | source)
XLA Modules:
  0.0 115.7 jit_solution(15992272891063334431)
XLA Ops:
  0.6 16.8 %first_half.1 = (bf16[2,4,4,4,16,128]{5,4,3,2,1,0:T(8,128)(2,1)}, f32[8,16,128]{2,1,0:T(8,128)}, f32[8,128]{1,0:T(8,128)}) custom-call(bf16[32,5120]{1,0:T(8,128)(2,1)} %bitcast.8, f32[1,5120]{1,0:T(1,128)} %bitcast.13, f32[1,128]{1,0:T(1,128)} %constant.2.clone.freq_ref, s32[1,128]{1,0:T(1,128)} %bitcast.15, s32[1,128]{1,0:T(1,128)} %bitcast.16, ...), custom_call_target="tpu_custom_call" | custom-call | tf_op jit(solution)/shard_map/first_half/pallas_call | solution.py:922
  17.4 12.4 %paged_attention.1 = (bf16[128,16,128]{2,1,0:T(8,128)(2,1)}, f32[128,128]{1,0:T(8,128)}) custom-call(s32[36]{0:T(128)} %request_ref.1, s32[36]{0:T(128)} %number_ref.1, s32[128]{0:T(128)} %slot_ref.1, s32[128]{0:T(128)} %length_ref.1, bf16[2,16,4,16,128]{4,3,2,1,0:T(8,128)(2,1)} %bitcast.10, bf16[36,1,256,128]{3,2,1,0:T(8,128)(2,1)} %k_ref.1, ...), custom_call_target="tpu_custom_call" | custom-call | tf_op jit(solution)/shard_map/paged_attention/pallas_call | solution.py:89
  29.8 84.0 %second_half.1 = (bf16[32,5120]{1,0:T(8,128)(2,1)}, bf16[32,5120]{1,0:T(8,128)(2,1)}) custom-call(bf16[16,8,16,128]{3,2,1,0:T(8,128)(2,1)} %bitcast.11, f32[16,8,128]{2,1,0:T(8,128)} %bitcast.12, f32[8,16,128]{2,1,0:T(8,128)} %get-tuple-element.12.fresh_ref, f32[8,128]{1,0:T(8,128)} %get-tuple-element.13.fresh_lse_ref, bf16[32,5120]{1,0:T(8,128)(2,1)} %bitcast.9, ...), custom_call_target="tpu_custom_call" | custom-call | tf_op jit(solution)/shard_map/second_half/pallas_call | solution.py:746
  113.8 1.9 %finish.1 = (bf16[4,8,5120]{2,1,0:T(8,128)(2,1)}, bf16[4,8,5120]{2,1,0:T(8,128)(2,1)}) custom-call(bf16[32,5120]{1,0:T(8,128)(2,1)} %get-tuple-element.14.a_ref, bf16[32,5120]{1,0:T(8,128)(2,1)} %get-tuple-element.15.b_ref), custom_call_target="tpu_custom_call" | custom-call | tf_op jit(solution)/shard_map/finish/pallas_call | solution.py:954

commit v9 on v8

--- a/solution.py
+++ b/solution.py
@@ -513,7 +513,7 @@
 
     use_slab(0, core)
     for db in (0, 3, 1, 2):
-        for g in gathers:
+        for g in (gathers[2], gathers[1], gathers[0]):
             g.space_near(db)
     use_slab(3, core)
     use_slab(1, core)
@@ -630,10 +630,11 @@
     slots_a = [[wire.slot() for _ in range(3)] for _ in range(3)]
     for s in along_c:
         s.open()
-    for s in along_c:
-        s.pass_on(2)
-    for k, s in enumerate(along_c):
-        s.close()
+    order = (2, 0, 1)
+    for k in order:
+        along_c[k].pass_on(2)
+    for k in order:
+        along_c[k].close()
         at = place.at[AXES[k][2]]
 
         def sum_c(b, carry):
@@ -652,7 +653,7 @@
                 nbs[k].at[j - 1],
                 place.device(axis, j),
             )
-    for k in range(3):
+    for k in order:
         axis = AXES[k][1]
         at = place.at[axis]
         for j in (1, 3, 2):
@@ -670,7 +671,7 @@
                 ras[k].at[j - 1],
                 place.device(axis, j),
             )
-    for k in range(3):
+    for k in order:
         axis = AXES[k][0]
         v = tas[k][place.at[axis]].astype(jnp.float32)
         for j in (1, 3, 2):

time: 116 us -> 116 us (level)
  no operation moved by 1% of the time
where the time goes in v9:
time: 116 us; the launch traced here: 115 us
  Pallas kernels  115 us (99%)
    pallas_call x1, Pallas kernels, second_half(): pl.pallas_call(functools.partial(block_kernel, widths), out_shape=[out, o...  83.8 us
    pallas_call x1, Pallas kernels, first_half(): pl.pallas_call(project_kernel, out_shape=[jax.ShapeDtypeStruct((2, 4, 4,...  16.8 us
    pallas_call x1, Pallas kernels, paged_attention(): pl.pallas_call(functools.partial(paged_kernel, pages), grid_spec=pltpu.Pr...  12.4 us

profile of v9, /device:TPU:1, one launch (start us, length us, event | category | flops | bytes accessed | tf_op | source)
XLA Modules:
  0.0 115.5 jit_solution(10928663856090311550)
XLA Ops:
  0.6 16.8 %first_half.1 = (bf16[2,4,4,4,16,128]{5,4,3,2,1,0:T(8,128)(2,1)}, f32[8,16,128]{2,1,0:T(8,128)}, f32[8,128]{1,0:T(8,128)}) custom-call(bf16[32,5120]{1,0:T(8,128)(2,1)} %bitcast.8, f32[1,5120]{1,0:T(1,128)} %bitcast.13, f32[1,128]{1,0:T(1,128)} %constant.2.clone.freq_ref, s32[1,128]{1,0:T(1,128)} %bitcast.15, s32[1,128]{1,0:T(1,128)} %bitcast.16, ...), custom_call_target="tpu_custom_call" | custom-call | tf_op jit(solution)/shard_map/first_half/pallas_call | solution.py:923
  17.4 12.4 %paged_attention.1 = (bf16[128,16,128]{2,1,0:T(8,128)(2,1)}, f32[128,128]{1,0:T(8,128)}) custom-call(s32[36]{0:T(128)} %request_ref.1, s32[36]{0:T(128)} %number_ref.1, s32[128]{0:T(128)} %slot_ref.1, s32[128]{0:T(128)} %length_ref.1, bf16[2,16,4,16,128]{4,3,2,1,0:T(8,128)(2,1)} %bitcast.10, bf16[36,1,256,128]{3,2,1,0:T(8,128)(2,1)} %k_ref.1, ...), custom_call_target="tpu_custom_call" | custom-call | tf_op jit(solution)/shard_map/paged_attention/pallas_call | solution.py:89
  29.8 83.8 %second_half.1 = (bf16[32,5120]{1,0:T(8,128)(2,1)}, bf16[32,5120]{1,0:T(8,128)(2,1)}) custom-call(bf16[16,8,16,128]{3,2,1,0:T(8,128)(2,1)} %bitcast.11, f32[16,8,128]{2,1,0:T(8,128)} %bitcast.12, f32[8,16,128]{2,1,0:T(8,128)} %get-tuple-element.12.fresh_ref, f32[8,128]{1,0:T(8,128)} %get-tuple-element.13.fresh_lse_ref, bf16[32,5120]{1,0:T(8,128)(2,1)} %bitcast.9, ...), custom_call_target="tpu_custom_call" | custom-call | tf_op jit(solution)/shard_map/second_half/pallas_call | solution.py:747
  113.6 1.9 %finish.1 = (bf16[4,8,5120]{2,1,0:T(8,128)(2,1)}, bf16[4,8,5120]{2,1,0:T(8,128)(2,1)}) custom-call(bf16[32,5120]{1,0:T(8,128)(2,1)} %get-tuple-element.14.a_ref, bf16[32,5120]{1,0:T(8,128)(2,1)} %get-tuple-element.15.b_ref), custom_call_target="tpu_custom_call" | custom-call | tf_op jit(solution)/shard_map/finish/pallas_call | solution.py:955
